TPU v7x, 256 devices: a whole 4x4x8 slice. The times are simulated.
256 devices in a mesh: blk: 8 (over x_hi, y), grp: 32 (over z, x_lo, core).
Axes of the slice: x: 4 (x_hi: 2, x_lo: 2; x = x_hi * 2 + x_lo), y: 4, z: 8, core: 2. Of those that a mesh axis runs over, the one named last changes fastest.
Arguments:
- amplitudes: bfloat16 [4, 4096, 1024], P(None, 'blk'), may hold values from -6 to 6
- pair_screen: int32 [4, 256], P(None, 'blk'), may hold values 0 or 1
- integrals: bfloat16 [256, 1024, 1024], P(('blk', 'grp')), may hold values from -0.1875 to 0.1875
- tile_ab: int32 [8, 32], replicated, may hold values from 0 to 49, as said below
- tile_cd: int32 [8, 32], replicated, may hold values from 0 to 3
- residual_in: float32 [4096, 50, 1024], P(('blk', 'grp')), may hold values from -6 to 6
Outputs:
- residual: float32 [4096, 50, 1024], P(('blk', 'grp'))
Inputs may be any that keep to these rules, and one draw needn't show every extreme that they name: `tile_ab`: the 8 integral tiles that share a column g name 2 to 4 distinct b tiles, and in every draw some column names exactly 4.
All inputs are finite; a program needn't handle non-finite values. No bound on the sum of `pair_screen` on one device may be relied on, other than what follows from the above.
Results may differ from a plain program's by a relative error of at most 0.0003.
Values may be sent and summed in bfloat16 or wider, within the bound.
A program may use at most 128 MiB of HBM per device.

v0:
```python
import jax
import jax.numpy as jnp
from jax import lax
from jax.sharding import PartitionSpec as P


def contract(masked, panel, cd_index):
    rows_in = lax.dynamic_index_in_dim(masked, cd_index, 0, keepdims=False)
    return jnp.dot(rows_in, panel, preferred_element_type=jnp.float32)


def shards(amplitudes, pair_screen, integrals, tile_ab, tile_cd, residual_in):
    blk_count = lax.axis_size("blk")
    grp_count = lax.axis_size("grp")
    grp_position = lax.axis_index("grp")
    owner_rows, ab_tiles, tile_width = residual_in.shape
    group_rows = amplitudes.shape[1]
    row_mask = jnp.repeat(pair_screen, owner_rows, axis=1).astype(jnp.bfloat16)
    masked = amplitudes * row_mask[:, :, None]
    column_cd = lax.dynamic_index_in_dim(tile_cd, grp_position, 1, keepdims=False)
    initial = jnp.zeros((blk_count, group_rows, tile_width), jnp.float32)
    running = initial
    portion = lax.all_gather(integrals, "blk", axis=0, tiled=True)
    first_row = jnp.int32(0)
    for offset in range(portion.shape[0]):
        position = first_row + offset
        product = contract(masked, portion[offset], column_cd[position])
        earlier = lax.dynamic_index_in_dim(running, position, 0, keepdims=False)
        running = lax.dynamic_update_index_in_dim(running, earlier + product, position, 0)
    arrived = lax.all_to_all(
        running.reshape(blk_count, grp_count, owner_rows, tile_width),
        "grp",
        split_axis=1,
        concat_axis=1,
        tiled=True,
    )
    blocks = arrived.reshape(blk_count * grp_count, owner_rows, tile_width)
    summed = jax.ops.segment_sum(blocks, tile_ab.reshape(-1), num_segments=ab_tiles)
    return residual_in + jnp.transpose(summed, (1, 0, 2))


def solution(mesh):
    in_specs = (
        P(None, "blk", None),
        P(None, "blk"),
        P(("blk", "grp"), None, None),
        P(),
        P(),
        P(("blk", "grp"), None, None),
    )
    out_specs = P(("blk", "grp"), None, None)
    return jax.shard_map(shards, mesh=mesh, in_specs=in_specs, out_specs=out_specs, check_vma=False)
```

profile of v0, /device:TPU:1, one launch (start us, length us, event | category | flops | bytes accessed | tf_op | source)
XLA Modules:
  0.0 665.4 jit_solution(16842557695121433719)
XLA Ops:
  6.5 0.0 copy-start
  6.5 0.0 all-gather.2.cloned.1.call-start
  6.5 0.7 all-gather.2.cloned.1.call-update
  7.3 0.0 copy-done
  7.3 0.1 constant_dynamic-slice_fusion
  7.3 0.6 fusion.51
  18.0 0.7 convert_element_type.11
  18.7 0.1 broadcast_in_dim.34
  18.8 0.1 convert_element_type.12
  23.9 4.9 broadcast_multiply_fusion
  28.8 172.5 %all-gather.2.cloned.1.call-done = bf16[8,1024,1024]{2,1,0:T(8,128)(2,1)} async-done(((bf16[1,1024,1024]{2,1,0:T(8,128)(2,1)}), bf16[8,1024,1024]{2,1,0:T(8,128)(2,1)}) %all-gather.2.cloned.1.call-update) | async-done | bytes 16777232 | tf_op jit(solution)/shard_map/all_gather | solution.py:23
  201.2 3.2 fusion.26
  204.4 2.2 dynamic_update_slice.25
  206.7 0.0 copy-start.2
  206.7 3.3 bitcast_dynamic-update-slice_fusion
  210.0 0.0 copy-done.2
  210.0 3.0 fusion.23
  213.0 3.0 fusion.19
  216.0 3.0 fusion.15
  219.0 3.0 fusion.11
  222.1 3.0 fusion.7
  225.1 3.0 fusion.3
  228.1 6.1 copy.8
  234.2 0.0 copy-start.3
  234.2 8.4 %all-to-all-start = ((f32[8,32,16,1024]{3,2,0,1:T(8,128)}), f32[8,32,16,1024]{3,2,0,1:T(8,128)}, u32[]{:S(2)}, u32[]{:S(2)}) async-start(f32[8,32,16,1024]{3,2,0,1:T(8,128)} %copy.8), calls=%async_computation | async-start | bytes 33554432 | tf_op jit(solution)/shard_map/all_to_all | solution.py:30
  242.6 0.0 copy-done.3
  242.6 0.1 reshape.33
  242.7 366.0 %all-to-all-done = f32[8,32,16,1024]{3,2,0,1:T(8,128)} async-done(((f32[8,32,16,1024]{3,2,0,1:T(8,128)}), f32[8,32,16,1024]{3,2,0,1:T(8,128)}, u32[]{:S(2)}, u32[]{:S(2)}) %all-to-all-start) | async-done | bytes 16777248 | tf_op jit(solution)/shard_map/all_to_all | solution.py:30
  608.7 11.8 %copy.9 = f32[8,32,16,1024]{3,2,1,0:T(8,128)} copy(f32[8,32,16,1024]{3,2,0,1:T(8,128)} %all-to-all-done) | data formatting | bytes 33554432 | tf_op jit(solution)/shard_map/all_to_all | solution.py:30
  620.5 0.4 broadcast_in_dim.33
  620.9 0.0 copy-start.1
  621.0 33.2 %scatter_fusion = f32[50,16,1024]{2,1,0:T(8,128)S(1)} fusion(f32[50,16,1024]{2,1,0:T(8,128)S(1)} %broadcast_in_dim.33, s32[256]{0:T(256)S(1)} %reshape.33, f32[256,16,1024]{2,1,0:T(8,128)} %bitcast.152), kind=kCustom, calls=%fused_computation | custom fusion | flops 4194304 | bytes 50332672 | tf_op jit(solution)/shard_map/scatter-add | solution.py:38
  654.2 4.4 bitcast_add_fusion
  658.6 0.0 copy-done.1
Async XLA Ops:
  6.5 0.7 copy-start
  6.5 194.7 %all-gather.2.cloned.1.call-start = ((), (), s32[]{:S(2)}) async-start(), calls=%async_computation.1 | async-start | bytes 18874368 | tf_op jit(solution)/shard_map/all_gather | solution.py:23
  206.7 3.3 copy-start.2
  234.2 8.4 %copy-start.3 = (s32[8,32]{1,0:T(8,128)S(1)}, s32[8,32]{1,0:T(8,128)}, u32[]{:S(2)}) copy-start(s32[8,32]{1,0:T(8,128)} %param.9) | copy-start | bytes 3076
  234.2 374.5 %all-to-all-start = ((f32[8,32,16,1024]{3,2,0,1:T(8,128)}), f32[8,32,16,1024]{3,2,0,1:T(8,128)}, u32[]{:S(2)}, u32[]{:S(2)}) async-start(f32[8,32,16,1024]{3,2,0,1:T(8,128)} %copy.8), calls=%async_computation | async-start | bytes 33554432 | tf_op jit(solution)/shard_map/all_to_all | solution.py:30
  620.9 37.6 %copy-start.1 = (s32[8,32]{1,0:T(8,128)S(1)}, s32[8,32]{1,0:T(8,128)}, u32[]{:S(2)}) copy-start(s32[8,32]{1,0:T(8,128)} %param.10) | copy-start | bytes 3076
Sparse Core Ops, SparseCore 0:
  10.0 191.1 all-gather.1
where the time goes:
time: 667 us; the launch traced here: 665 us
  waiting for transfers between devices  539 us (81%)
  other arithmetic  43.2 us (6%)
  between operations  28.6 us (4%)
  matrix products  24.6 us (4%)
  local copies, waits for them, and re-layouts  21.5 us (3%)
  starting transfers between devices  8.44 us (1%)
    all_to_all x1, waiting for transfers between devices, shards(): lax.all_to_all(running.reshape(blk_count, grp_count, owner_rows, tile_wid...  366 us
    all_gather x1, waiting for transfers between devices, shards(): portion = lax.all_gather(integrals, 'blk', axis=0, tiled=True)  172 us
    scatter-add x1, other arithmetic, shards(): jax.ops.segment_sum(blocks, tile_ab.reshape(-1), num_segments=ab_tiles)  33.2 us
    dot_general x8, matrix products, contract(): return jnp.dot(rows_in, panel, preferred_element_type=jnp.float32)  24.6 us
  transfers between devices with their start and end apart: 2, of which 2 were waited for; matrix products, arithmetic and copies ran while one was open for 1% of the time, Pallas kernels for 0%

commit v1 on v0

v1 whole, which is shorter than its diff:
```python
import jax
import jax.numpy as jnp
from jax import lax
from jax.sharding import PartitionSpec as P

SLOTS = 4


def slot_of(column_ab):
    tiles = column_ab.shape[0]
    order = jnp.arange(tiles).reshape((tiles,) + (1,) * (column_ab.ndim - 1))
    same = column_ab[:, None] == column_ab[None, :]
    first = jnp.argmax(same, axis=1)
    is_first = first == order
    earlier = order[None, :] < first[:, None]
    return jnp.sum(earlier & is_first[None, :], axis=1).astype(jnp.int32)


def shards(amplitudes, pair_screen, integrals, tile_ab, tile_cd, residual_in):
    grp_count = lax.axis_size("grp")
    grp_position = lax.axis_index("grp")
    owner_rows, ab_tiles, tile_width = residual_in.shape
    group_rows = amplitudes.shape[1]
    row_mask = jnp.repeat(pair_screen, owner_rows, axis=1).astype(jnp.bfloat16)
    masked = amplitudes * row_mask[:, :, None]
    column_cd = lax.dynamic_index_in_dim(tile_cd, grp_position, 1, keepdims=False)
    column_ab = lax.dynamic_index_in_dim(tile_ab, grp_position, 1, keepdims=False)
    column_slot = slot_of(column_ab)
    portion = lax.all_gather(integrals, "blk", axis=0, tiled=True)
    running = jnp.zeros((SLOTS, group_rows, tile_width), jnp.float32)
    for offset in range(portion.shape[0]):
        rows_in = lax.dynamic_index_in_dim(masked, column_cd[offset], 0, keepdims=False)
        product = jnp.dot(rows_in, portion[offset], preferred_element_type=jnp.float32)
        slot = column_slot[offset]
        earlier = lax.dynamic_index_in_dim(running, slot, 0, keepdims=False)
        running = lax.dynamic_update_index_in_dim(running, earlier + product, slot, 0)
    arrived = lax.all_to_all(
        running.reshape(SLOTS, grp_count, owner_rows, tile_width),
        "grp",
        split_axis=1,
        concat_axis=1,
        tiled=True,
    )
    all_slot = slot_of(tile_ab)
    slot_hit = all_slot[:, None, :] == jnp.arange(SLOTS)[None, :, None]
    ab_hit = tile_ab[None, :, :] == jnp.arange(ab_tiles)[:, None, None]
    onehot = jnp.any(ab_hit[:, :, None, :] & slot_hit[None, :, :, :], axis=1).astype(jnp.float32)
    summed = jnp.einsum(
        "nsg,sgrc->rnc", onehot, arrived, precision=lax.Precision.HIGHEST, preferred_element_type=jnp.float32
    )
    return residual_in + summed


def solution(mesh):
    in_specs = (
        P(None, "blk", None),
        P(None, "blk"),
        P(("blk", "grp"), None, None),
        P(),
        P(),
        P(("blk", "grp"), None, None),
    )
    out_specs = P(("blk", "grp"), None, None)
    return jax.shard_map(shards, mesh=mesh, in_specs=in_specs, out_specs=out_specs, check_vma=False)
```

time: 667 us -> 474 us (0.71)
  waiting for transfers between devices: 539 us -> 342 us
  other arithmetic: 43.2 us -> 10.9 us
  between operations: 28.6 us -> 43.5 us
  local copies, waits for them, and re-layouts: 21.5 us -> 33.9 us
  matrix products: 24.6 us -> 34.6 us
    all_to_all x1, waiting for transfers between devices: 366 us -> 186 us  [shards(): lax.all_to_all(running.reshape(SLOTS, grp_count, owner_rows, tile_width),...]
    scatter-add x1 -> x0, other arithmetic: 33.2 us -> none  [shards(): jax.ops.segment_sum(blocks, tile_ab.reshape(-1), num_segments=ab_tiles)]
    all_gather x1, waiting for transfers between devices: 172 us -> 156 us  [shards(): portion = lax.all_gather(integrals, 'blk', axis=0, tiled=True)]
    all_to_all x1 -> x0, local copies, waits for them, and re-layouts: 11.8 us -> none  [shards(): lax.all_to_all(running.reshape(blk_count, grp_count, owner_rows, tile_wid...]
    dynamic_slice x1 -> x7, local copies, waits for them, and re-layouts: 0.61 us -> 12.3 us  [shards(): earlier = lax.dynamic_index_in_dim(running, slot, 0, keepdims=False)]
    dot_general x8 -> x9, matrix products: 24.6 us -> 34.6 us  [the longest x8 23.1 us: shards(): jnp.dot(rows_in, portion[offset], preferred_element_type=jnp.float32)]
    reshape x1, local copies, waits for them, and re-layouts: 6.06 us -> 14 us  [shards(): running.reshape(SLOTS, grp_count, owner_rows, tile_width)]
  transfers between devices with their start and end apart: 2 -> 2, of which waited for: 2 -> 2; matrix products, arithmetic and copies ran while one was open for 1% -> 2% of each run, Pallas kernels for 0% -> 0%
where the time goes in v1:
time: 474 us; the launch traced here: 473 us
  waiting for transfers between devices  342 us (72%)
  between operations  43.5 us (9%)
  matrix products  34.6 us (7%)
  local copies, waits for them, and re-layouts  33.9 us (7%)
  other arithmetic  10.9 us (2%)
  starting transfers between devices  8.63 us (2%)
    all_to_all x1, waiting for transfers between devices, shards(): lax.all_to_all(running.reshape(SLOTS, grp_count, owner_rows, tile_width),...  186 us
    all_gather x1, waiting for transfers between devices, shards(): portion = lax.all_gather(integrals, 'blk', axis=0, tiled=True)  156 us
    dot_general x8, matrix products, shards(): jnp.dot(rows_in, portion[offset], preferred_element_type=jnp.float32)  23.1 us
    reshape x1, local copies, waits for them, and re-layouts, shards(): running.reshape(SLOTS, grp_count, owner_rows, tile_width)  14 us
    dynamic_slice x7, local copies, waits for them, and re-layouts, shards(): earlier = lax.dynamic_index_in_dim(running, slot, 0, keepdims=False)  12.3 us
    dot_general x1, matrix products, shards(): jnp.einsum('nsg,sgrc->rnc', onehot, arrived, precision=lax.Precision.HIGH...  11.5 us
  transfers between devices with their start and end apart: 2, of which 2 were waited for; matrix products, arithmetic and copies ran while one was open for 2% of the time, Pallas kernels for 0%

profile of v1, /device:TPU:1, one launch (start us, length us, event | category | flops | bytes accessed | tf_op | source)
XLA Modules:
  0.0 473.3 jit_solution(12704014323719439289)
XLA Ops:
  6.5 0.0 all-gather.2.cloned.1.call-start
  6.5 0.7 all-gather.2.cloned.1.call-update
  7.3 0.9 constant_dynamic-slice_fusion.8
  8.2 0.7 iota_reduce_fusion.1
  8.9 0.2 convert_reduce_fusion.1
  9.0 0.7 fusion.42
  11.1 0.6 fusion.41
  30.3 0.7 convert_element_type.18
  31.0 0.1 broadcast_in_dim.48
  31.1 0.1 convert_element_type.19
  41.2 4.5 broadcast_multiply_fusion
  45.7 155.5 %all-gather.2.cloned.1.call-done = bf16[8,1024,1024]{2,1,0:T(8,128)(2,1)} async-done(((bf16[1,1024,1024]{2,1,0:T(8,128)(2,1)}), bf16[8,1024,1024]{2,1,0:T(8,128)(2,1)}) %all-gather.2.cloned.1.call-update) | async-done | bytes 16777232 | tf_op jit(solution)/shard_map/all_gather | solution.py:29
  201.2 0.0 copy-start
  201.2 0.0 copy-start.3
  201.2 5.3 %broadcast_in_dim.47 = f32[4,512,1024]{2,1,0:T(8,128)} broadcast(f32[]{:T(128)} %constant.74.clone.1), dimensions={} | broadcast | bytes 8388612 | tf_op jit(solution)/shard_map/broadcast_in_dim | solution.py:30
  206.6 0.0 copy-done
  206.6 4.9 %bitcast_dynamic-update-slice_fusion.7 = f32[4,512,1024]{2,1,0:T(8,128)} fusion(f32[4,512,1024]{2,1,0:T(8,128)} %broadcast_in_dim.47, s32[]{:T(128)S(6)} %select_n.74, bf16[8,1024,1024]{2,1,0:T(8,128)(2,1)} %all-gather.2.cloned.1.call-done, bf16[4,512,1024]{2,1,0:T(8,128)(2,1)S(1)} %copy-done, s32[]{:T(128)S(6)} %select_n.73), kind=kOutput, calls=%fused_computation.33 | convolution fusion | flops 1073741824 | bytes 5242888 | tf_op jit(solution)/shard_map/dot_general | solution.py:33
  211.5 1.9 constant_dynamic-slice_fusion.6
  213.4 0.0 copy-done.3
  213.4 2.6 bitcast_dynamic-update-slice_fusion.6
  216.0 1.7 constant_dynamic-slice_fusion.4
  217.7 2.6 bitcast_dynamic-update-slice_fusion.5
  220.3 1.7 constant_dynamic-slice_fusion.3
  222.1 2.6 bitcast_dynamic-update-slice_fusion.4
  224.7 1.7 constant_dynamic-slice_fusion.2
  226.4 2.6 bitcast_dynamic-update-slice_fusion.3
  229.0 1.7 constant_dynamic-slice_fusion.1
  230.8 2.6 bitcast_dynamic-update-slice_fusion.2
  233.4 1.7 constant_dynamic-slice_fusion
  235.1 2.6 bitcast_dynamic-update-slice_fusion.1
  237.7 1.7 constant_dynamic-slice_fusion.5
  239.4 2.6 bitcast_dynamic-update-slice_fusion
  242.0 14.0 %copy.20 = f32[4,32,16,1024]{3,0,2,1:T(4,128)} copy(f32[4,32,16,1024]{3,2,1,0:T(8,128)} %bitcast.47) | data formatting | bytes 16777216 | tf_op jit(solution)/shard_map/reshape | solution.py:38
  255.9 0.0 copy-start.2
  255.9 8.6 %all-to-all-start = ((f32[4,32,16,1024]{3,0,2,1:T(4,128)}), f32[4,32,16,1024]{3,0,2,1:T(4,128)}, u32[]{:S(2)}, u32[]{:S(2)}) async-start(f32[4,32,16,1024]{3,0,2,1:T(4,128)} %copy.20), calls=%async_computation | async-start | bytes 16777216 | tf_op jit(solution)/shard_map/all_to_all | solution.py:37
  264.6 0.0 copy-done.2
  264.6 0.6 iota_reduce_fusion
  265.2 0.1 iota_compare_fusion
  265.3 0.2 and_reduce_fusion
  265.5 0.0 copy-start.1
  265.6 185.6 %all-to-all-done = f32[4,32,16,1024]{3,0,2,1:T(4,128)} async-done(((f32[4,32,16,1024]{3,0,2,1:T(4,128)}), f32[4,32,16,1024]{3,0,2,1:T(4,128)}, u32[]{:S(2)}, u32[]{:S(2)}) %all-to-all-start) | async-done | bytes 8388640 | tf_op jit(solution)/shard_map/all_to_all | solution.py:37
  451.2 11.5 %fusion.10 = f32[16,1024,50]{1,2,0:T(8,128)S(1)} fusion(f32[4,32,16,1024]{3,0,2,1:T(4,128)} %all-to-all-done, pred[50,4,32]{0,2,1:T(8,128)(4,1)S(1)} %and_reduce_fusion), kind=kOutput, calls=%fused_computation.35 | convolution fusion | flops 1258291200 | bytes 11671808 | tf_op jit(solution)/shard_map/nsg,sgrc->rnc/dot_general | solution.py:48
  462.6 0.0 copy-done.1
  462.7 3.8 bitcast_add_fusion
  (4 shorter events, 0.0 us)
Async XLA Ops:
  6.5 194.7 %all-gather.2.cloned.1.call-start = ((), (), s32[]{:S(2)}) async-start(), calls=%async_computation.1 | async-start | bytes 18874368 | tf_op jit(solution)/shard_map/all_gather | solution.py:29
  201.2 5.3 %copy-start = (bf16[4,512,1024]{2,1,0:T(8,128)(2,1)S(1)}, bf16[4,512,1024]{2,1,0:T(8,128)(2,1)}, u32[]{:S(2)}) copy-start(bf16[4,512,1024]{2,1,0:T(8,128)(2,1)} %broadcast_multiply_fusion) | copy-start | bytes 12582916
  201.2 12.2 %copy-start.3 = (bf16[8,1024,1024]{2,1,0:T(8,128)(2,1)S(1)}, bf16[8,1024,1024]{2,1,0:T(8,128)(2,1)}, u32[]{:S(2)}) copy-start(bf16[8,1024,1024]{2,1,0:T(8,128)(2,1)} %all-gather.2.cloned.1.call-done) | copy-start | bytes 50331652
  255.9 8.6 %copy-start.2 = (s32[8,32]{1,0:T(8,128)S(1)}, s32[8,32]{1,0:T(8,128)}, u32[]{:S(2)}) copy-start(s32[8,32]{1,0:T(8,128)} %param.9) | copy-start | bytes 3076
  255.9 195.2 %all-to-all-start = ((f32[4,32,16,1024]{3,0,2,1:T(4,128)}), f32[4,32,16,1024]{3,0,2,1:T(4,128)}, u32[]{:S(2)}, u32[]{:S(2)}) async-start(f32[4,32,16,1024]{3,0,2,1:T(4,128)} %copy.20), calls=%async_computation | async-start | bytes 16777216 | tf_op jit(solution)/shard_map/all_to_all | solution.py:37
  265.5 197.1 %copy-start.1 = (f32[16,50,1024]{2,0,1:T(8,128)S(1)}, f32[16,50,1024]{2,0,1:T(8,128)}, u32[]{:S(2)}) copy-start(f32[16,50,1024]{2,0,1:T(8,128)} %param.11) | copy-start | bytes 9830404
Sparse Core Ops, SparseCore 0:
  10.0 191.1 all-gather.1

commit v2 on v1

--- a/solution.py
+++ b/solution.py
@@ -4,6 +4,7 @@
 from jax.sharding import PartitionSpec as P
 
 SLOTS = 4
+CHUNKS = 4
 
 
 def slot_of(column_ab):
@@ -26,28 +27,35 @@
     column_cd = lax.dynamic_index_in_dim(tile_cd, grp_position, 1, keepdims=False)
     column_ab = lax.dynamic_index_in_dim(tile_ab, grp_position, 1, keepdims=False)
     column_slot = slot_of(column_ab)
-    portion = lax.all_gather(integrals, "blk", axis=0, tiled=True)
-    running = jnp.zeros((SLOTS, group_rows, tile_width), jnp.float32)
-    for offset in range(portion.shape[0]):
-        rows_in = lax.dynamic_index_in_dim(masked, column_cd[offset], 0, keepdims=False)
-        product = jnp.dot(rows_in, portion[offset], preferred_element_type=jnp.float32)
-        slot = column_slot[offset]
-        earlier = lax.dynamic_index_in_dim(running, slot, 0, keepdims=False)
-        running = lax.dynamic_update_index_in_dim(running, earlier + product, slot, 0)
-    arrived = lax.all_to_all(
-        running.reshape(SLOTS, grp_count, owner_rows, tile_width),
-        "grp",
-        split_axis=1,
-        concat_axis=1,
-        tiled=True,
-    )
     all_slot = slot_of(tile_ab)
     slot_hit = all_slot[:, None, :] == jnp.arange(SLOTS)[None, :, None]
     ab_hit = tile_ab[None, :, :] == jnp.arange(ab_tiles)[:, None, None]
     onehot = jnp.any(ab_hit[:, :, None, :] & slot_hit[None, :, :, :], axis=1).astype(jnp.float32)
-    summed = jnp.einsum(
-        "nsg,sgrc->rnc", onehot, arrived, precision=lax.Precision.HIGHEST, preferred_element_type=jnp.float32
-    )
+    chunk = tile_width // CHUNKS
+    pieces = []
+    for part in range(CHUNKS):
+        columns = slice(part * chunk, (part + 1) * chunk)
+        portion = lax.all_gather(integrals[:, :, columns], "blk", axis=0, tiled=True)
+        running = jnp.zeros((SLOTS, group_rows, chunk), jnp.float32)
+        for offset in range(portion.shape[0]):
+            rows_in = lax.dynamic_index_in_dim(masked, column_cd[offset], 0, keepdims=False)
+            product = jnp.dot(rows_in, portion[offset], preferred_element_type=jnp.float32)
+            slot = column_slot[offset]
+            earlier = lax.dynamic_index_in_dim(running, slot, 0, keepdims=False)
+            running = lax.dynamic_update_index_in_dim(running, earlier + product, slot, 0)
+        arrived = lax.all_to_all(
+            running.reshape(SLOTS, grp_count, owner_rows, chunk),
+            "grp",
+            split_axis=1,
+            concat_axis=1,
+            tiled=True,
+        )
+        pieces.append(
+            jnp.einsum(
+                "nsg,sgrc->rnc", onehot, arrived, precision=lax.Precision.HIGHEST, preferred_element_type=jnp.float32
+            )
+        )
+    summed = jnp.concatenate(pieces, axis=2)
     return residual_in + summed
 
 

time: 474 us -> 447 us (0.943)
  waiting for transfers between devices: 342 us -> 303 us
  starting transfers between devices: 8.63 us -> 29.3 us
  local copies, waits for them, and re-layouts: 33.9 us -> 22.6 us
    all_to_all x1 -> x4, waiting for transfers between devices: 186 us -> 39.2 us  [shards(): lax.all_to_all(running.reshape(SLOTS, grp_count, owner_rows, chunk), 'grp...]
    all_gather x1 -> x4, waiting for transfers between devices: 156 us -> 262 us  [shards(): lax.all_gather(integrals[:, :, columns], 'blk', axis=0, tiled=True)]
    all_to_all x1 -> x4, starting transfers between devices: 8.63 us -> 29 us  [shards(): lax.all_to_all(running.reshape(SLOTS, grp_count, owner_rows, chunk), 'grp...]
    dynamic_slice x7 -> x28, local copies, waits for them, and re-layouts: 12.3 us -> 1.21 us  [shards(): earlier = lax.dynamic_index_in_dim(running, slot, 0, keepdims=False)]
    broadcast_in_dim x1 -> x0, local copies, waits for them, and re-layouts: 5.32 us -> none  [shards(): running = jnp.zeros((SLOTS, group_rows, tile_width), jnp.float32)]
    dot_general x8 -> x32, matrix products: 23.1 us -> 25.4 us  [shards(): jnp.dot(rows_in, portion[offset], preferred_element_type=jnp.float32)]
    reshape x1 -> x4, local copies, waits for them, and re-layouts: 14 us -> 12.4 us  [shards(): running.reshape(SLOTS, grp_count, owner_rows, chunk)]
    dot_general x1 -> x4, matrix products: 11.5 us -> 12.8 us  [shards(): jnp.einsum('nsg,sgrc->rnc', onehot, arrived, precision=lax.Precision.HIGH...]
  transfers between devices with their start and end apart: 2 -> 8, of which waited for: 2 -> 5; matrix products, arithmetic and copies ran while one was open for 2% -> 13% of each run, Pallas kernels for 0% -> 0%
where the time goes in v2:
time: 447 us; the launch traced here: 446 us
  waiting for transfers between devices  303 us (68%)
  between operations  43.9 us (10%)
  matrix products  38.2 us (9%)
  starting transfers between devices  29.3 us (7%)
  local copies, waits for them, and re-layouts  22.6 us (5%)
  other arithmetic  8.84 us (2%)
    all_gather x4, waiting for transfers between devices, shards(): lax.all_gather(integrals[:, :, columns], 'blk', axis=0, tiled=True)  262 us
    all_to_all x4, waiting for transfers between devices, shards(): lax.all_to_all(running.reshape(SLOTS, grp_count, owner_rows, chunk), 'grp...  39.2 us
    all_to_all x4, starting transfers between devices, shards(): lax.all_to_all(running.reshape(SLOTS, grp_count, owner_rows, chunk), 'grp...  29 us
    dot_general x32, matrix products, shards(): jnp.dot(rows_in, portion[offset], preferred_element_type=jnp.float32)  25.4 us
    dot_general x4, matrix products, shards(): jnp.einsum('nsg,sgrc->rnc', onehot, arrived, precision=lax.Precision.HIGH...  12.8 us
    reshape x4, local copies, waits for them, and re-layouts, shards(): running.reshape(SLOTS, grp_count, owner_rows, chunk)  12.4 us
  transfers between devices with their start and end apart: 8, of which 5 were waited for; matrix products, arithmetic and copies ran while one was open for 13% of the time, Pallas kernels for 0%

profile of v2, /device:TPU:1, one launch (start us, length us, event | category | flops | bytes accessed | tf_op | source)
XLA Modules:
  0.0 446.2 jit_solution(8523653879021673629)
XLA Ops:
  6.5 2.9 fusion.183
  9.6 0.7 all-gather.7.cloned.1.call-update
  10.3 0.7 all-gather.9.cloned.1.call-update
  11.2 0.8 iota_reduce_fusion.1
  12.2 0.7 fusion.185
  14.1 0.6 fusion.184
  43.7 4.5 %broadcast_multiply_fusion = bf16[4,512,1024]{2,1,0:T(8,128)(2,1)} fusion(bf16[4,512,1024]{2,1,0:T(8,128)(2,1)} %param.6, bf16[4,512]{1,0:T(4,128)(2,1)S(1)} %convert_element_type.19), kind=kLoop, calls=%fused_computation.9 | loop fusion | flops 2097152 | bytes 8392704 | tf_op jit(solution)/shard_map/mul | solution.py:26
  48.2 41.7 %all-gather.5.cloned.1.call-done = bf16[8,1024,256]{2,1,0:T(8,128)(2,1)} async-done(((bf16[1,1024,256]{2,1,0:T(8,128)(2,1)}), bf16[8,1024,256]{2,1,0:T(8,128)(2,1)}) %all-gather.5.cloned.1.call-update) | async-done | bytes 4194320 | tf_op jit(solution)/shard_map/all_gather | solution.py:38
  90.1 1.9 fusion.79
  92.1 0.5 copy-done
  92.6 1.7 fusion.75
  95.5 0.4 fusion.69
  96.0 0.5 fusion.67
  97.1 0.4 fusion.63
  97.5 3.1 copy.35
  100.6 8.3 %all-to-all-start = ((f32[4,32,16,256]{3,0,2,1:T(4,128)}), f32[4,32,16,256]{3,0,2,1:T(4,128)S(1)}, u32[]{:S(2)}, u32[]{:S(2)}) async-start(f32[4,32,16,256]{3,0,2,1:T(4,128)} %copy.35), calls=%async_computation | async-start | bytes 4194304 | tf_op jit(solution)/shard_map/all_to_all | solution.py:46
  109.5 72.6 %all-gather.7.cloned.1.call-done = bf16[8,1024,256]{2,1,0:T(8,128)(2,1)} async-done(((bf16[1,1024,256]{2,1,0:T(8,128)(2,1)}), bf16[8,1024,256]{2,1,0:T(8,128)(2,1)}) %all-gather.7.cloned.1.call-update) | async-done | bytes 4194320 | tf_op jit(solution)/shard_map/all_gather | solution.py:38
  182.2 1.9 fusion.78
  184.3 0.5 copy-done.1
  184.7 1.7 fusion.61
  187.2 0.5 fusion.57
  188.7 0.5 fusion.51
  189.7 3.1 copy.38
  192.8 7.1 %all-to-all-start.1 = ((f32[4,32,16,256]{3,0,2,1:T(4,128)}), f32[4,32,16,256]{3,0,2,1:T(4,128)}, u32[]{:S(2)}, u32[]{:S(2)}) async-start(f32[4,32,16,256]{3,0,2,1:T(4,128)} %copy.38), calls=%async_computation.1 | async-start | bytes 4194304 | tf_op jit(solution)/shard_map/all_to_all | solution.py:46
  199.9 74.6 %all-gather.9.cloned.1.call-done = bf16[8,1024,256]{2,1,0:T(8,128)(2,1)} async-done(((bf16[1,1024,256]{2,1,0:T(8,128)(2,1)}), bf16[8,1024,256]{2,1,0:T(8,128)(2,1)}) %all-gather.9.cloned.1.call-update) | async-done | bytes 4194320 | tf_op jit(solution)/shard_map/all_gather | solution.py:38
  274.7 1.9 fusion.77
  276.7 0.5 copy-done.2
  277.2 1.7 fusion.47
  280.6 0.5 fusion.39
  281.1 0.5 fusion.37
  281.6 0.5 fusion.35
  282.1 3.1 copy.41
  285.2 6.8 %all-to-all-start.2 = ((f32[4,32,16,256]{3,0,2,1:T(4,128)}), f32[4,32,16,256]{3,0,2,1:T(4,128)}, u32[]{:S(2)}, u32[]{:S(2)}) async-start(f32[4,32,16,256]{3,0,2,1:T(4,128)} %copy.41), calls=%async_computation.2 | async-start | bytes 4194304 | tf_op jit(solution)/shard_map/all_to_all | solution.py:46
  292.1 73.4 %all-gather.11.cloned.1.call-done = bf16[8,1024,256]{2,1,0:T(8,128)(2,1)} async-done(((bf16[1,1024,256]{2,1,0:T(8,128)(2,1)}), bf16[8,1024,256]{2,1,0:T(8,128)(2,1)}) %all-gather.11.cloned.1.call-update) | async-done | bytes 4194320 | tf_op jit(solution)/shard_map/all_gather | solution.py:38
  365.7 2.0 fusion.76
  367.7 0.5 copy-done.3
  368.2 1.7 fusion.33
  370.6 0.5 fusion.29
  372.7 0.5 fusion.21
  373.1 3.1 copy.44
  376.2 6.8 %all-to-all-start.3 = ((f32[4,32,16,256]{3,0,2,1:T(4,128)}), f32[4,32,16,256]{3,0,2,1:T(4,128)}, u32[]{:S(2)}, u32[]{:S(2)}) async-start(f32[4,32,16,256]{3,0,2,1:T(4,128)} %copy.44), calls=%async_computation.3 | async-start | bytes 4194304 | tf_op jit(solution)/shard_map/all_to_all | solution.py:46
  383.1 0.6 iota_reduce_fusion
  384.0 2.1 fusion.8
  386.3 3.5 fusion.11
  390.2 3.5 fusion.14
  394.0 39.2 %all-to-all-done.3 = f32[4,32,16,256]{3,0,2,1:T(4,128)} async-done(((f32[4,32,16,256]{3,0,2,1:T(4,128)}), f32[4,32,16,256]{3,0,2,1:T(4,128)}, u32[]{:S(2)}, u32[]{:S(2)}) %all-to-all-start.3) | async-done | bytes 2097184 | tf_op jit(solution)/shard_map/all_to_all | solution.py:46
  433.2 3.7 fusion.17
  437.2 2.5 maximum_add_fusion
  (90 shorter events, 11.5 us)
Async XLA Ops:
  6.5 4.5 copy-start.10
  6.5 4.5 %copy-start.9 = (s32[8,32]{1,0:T(8,128)S(1)}, s32[8,32]{1,0:T(8,128)}, u32[]{:S(2)}) copy-start(s32[8,32]{1,0:T(8,128)} %param.9) | copy-start | bytes 3076
  6.5 27.0 %copy-start.11 = (s32[4,32]{1,0:T(4,128)S(1)}, s32[4,32]{1,0:T(4,128)}, u32[]{:S(2)}) copy-start(s32[4,32]{1,0:T(4,128)} %param.7) | copy-start | bytes 1540
  6.5 83.4 %all-gather.5.cloned.1.call-start = ((), (), s32[]{:S(2)}) async-start(), calls=%async_computation.4 | async-start | bytes 4718592 | tf_op jit(solution)/shard_map/all_gather | solution.py:38
  9.5 172.6 %all-gather.7.cloned.1.call-start = ((), (), s32[]{:S(2)}) async-start(), calls=%async_computation.5 | async-start | bytes 4718592 | tf_op jit(solution)/shard_map/all_gather | solution.py:38
  10.3 264.2 %all-gather.9.cloned.1.call-start = ((), (), s32[]{:S(2)}) async-start(), calls=%async_computation.6 | async-start | bytes 4718592 | tf_op jit(solution)/shard_map/all_gather | solution.py:38
  89.9 2.7 copy-start
  92.0 2.5 copy-start.7
  100.6 92.2 %all-to-all-start = ((f32[4,32,16,256]{3,0,2,1:T(4,128)}), f32[4,32,16,256]{3,0,2,1:T(4,128)S(1)}, u32[]{:S(2)}, u32[]{:S(2)}) async-start(f32[4,32,16,256]{3,0,2,1:T(4,128)} %copy.35), calls=%async_computation | async-start | bytes 4194304 | tf_op jit(solution)/shard_map/all_to_all | solution.py:46
  108.9 256.6 %all-gather.11.cloned.1.call-start = ((), (), s32[]{:S(2)}) async-start(), calls=%async_computation.7 | async-start | bytes 4718592 | tf_op jit(solution)/shard_map/all_gather | solution.py:38
  182.1 2.7 copy-start.1
  184.2 2.5 copy-start.6
  192.8 92.5 %all-to-all-start.1 = ((f32[4,32,16,256]{3,0,2,1:T(4,128)}), f32[4,32,16,256]{3,0,2,1:T(4,128)}, u32[]{:S(2)}, u32[]{:S(2)}) async-start(f32[4,32,16,256]{3,0,2,1:T(4,128)} %copy.38), calls=%async_computation.1 | async-start | bytes 4194304 | tf_op jit(solution)/shard_map/all_to_all | solution.py:46
  274.5 2.7 copy-start.2
  276.6 2.5 copy-start.5
  285.2 91.0 %all-to-all-start.2 = ((f32[4,32,16,256]{3,0,2,1:T(4,128)}), f32[4,32,16,256]{3,0,2,1:T(4,128)}, u32[]{:S(2)}, u32[]{:S(2)}) async-start(f32[4,32,16,256]{3,0,2,1:T(4,128)} %copy.41), calls=%async_computation.2 | async-start | bytes 4194304 | tf_op jit(solution)/shard_map/all_to_all | solution.py:46
  365.5 2.7 copy-start.3
  367.6 2.5 copy-start.8
  376.2 57.0 %all-to-all-start.3 = ((f32[4,32,16,256]{3,0,2,1:T(4,128)}), f32[4,32,16,256]{3,0,2,1:T(4,128)}, u32[]{:S(2)}, u32[]{:S(2)}) async-start(f32[4,32,16,256]{3,0,2,1:T(4,128)} %copy.44), calls=%async_computation.3 | async-start | bytes 4194304 | tf_op jit(solution)/shard_map/all_to_all | solution.py:46
  433.2 4.0 copy-start.4
Sparse Core Ops, SparseCore 0:
  10.0 79.8 all-gather.4
  92.6 89.4 all-gather.6
  184.7 89.7 all-gather.8
  277.0 88.4 all-gather.10

commit v3 on v2

--- a/solution.py
+++ b/solution.py
@@ -32,10 +32,10 @@
     ab_hit = tile_ab[None, :, :] == jnp.arange(ab_tiles)[:, None, None]
     onehot = jnp.any(ab_hit[:, :, None, :] & slot_hit[None, :, :, :], axis=1).astype(jnp.float32)
     chunk = tile_width // CHUNKS
+    chunked = jnp.transpose(integrals.reshape(integrals.shape[1], CHUNKS, chunk), (1, 0, 2))
     pieces = []
     for part in range(CHUNKS):
-        columns = slice(part * chunk, (part + 1) * chunk)
-        portion = lax.all_gather(integrals[:, :, columns], "blk", axis=0, tiled=True)
+        portion = lax.all_gather(chunked[part : part + 1], "blk", axis=0, tiled=True)
         running = jnp.zeros((SLOTS, group_rows, chunk), jnp.float32)
         for offset in range(portion.shape[0]):
             rows_in = lax.dynamic_index_in_dim(masked, column_cd[offset], 0, keepdims=False)

time: 447 us -> 450 us (level)
  local copies, waits for them, and re-layouts: 22.6 us -> 29.8 us
  transfers between devices with their start and end apart: 8 -> 8, of which waited for: 5 -> 5; matrix products, arithmetic and copies ran while one was open for 13% -> 14% of each run, Pallas kernels for 0% -> 0%
where the time goes in v3:
time: 450 us; the launch traced here: 449 us
  waiting for transfers between devices  299 us (66%)
  between operations  43.3 us (10%)
  matrix products  38.2 us (8%)
  local copies, waits for them, and re-layouts  29.8 us (7%)
  starting transfers between devices  29.4 us (7%)
  other arithmetic  8.83 us (2%)
    all_gather x4, waiting for transfers between devices, shards(): portion = lax.all_gather(chunked[part:part + 1], 'blk', axis=0, tiled=True)  260 us
    all_to_all x4, waiting for transfers between devices, shards(): lax.all_to_all(running.reshape(SLOTS, grp_count, owner_rows, chunk), 'grp...  39.2 us
    all_to_all x4, starting transfers between devices, shards(): lax.all_to_all(running.reshape(SLOTS, grp_count, owner_rows, chunk), 'grp...  29.1 us
    dot_general x32, matrix products, shards(): jnp.dot(rows_in, portion[offset], preferred_element_type=jnp.float32)  25.4 us
    dot_general x4, matrix products, shards(): jnp.einsum('nsg,sgrc->rnc', onehot, arrived, precision=lax.Precision.HIGH...  12.8 us
    reshape x4, local copies, waits for them, and re-layouts, shards(): running.reshape(SLOTS, grp_count, owner_rows, chunk)  12.4 us
  transfers between devices with their start and end apart: 8, of which 5 were waited for; matrix products, arithmetic and copies ran while one was open for 14% of the time, Pallas kernels for 0%

profile of v3, /device:TPU:1, one launch (start us, length us, event | category | flops | bytes accessed | tf_op | source)
XLA Modules:
  0.0 449.0 jit_solution(1546076032682252925)
XLA Ops:
  6.5 2.9 copy.84
  9.4 1.2 fusion.183
  10.6 2.0 copy.85
  12.7 2.0 copy.89
  14.9 1.0 copy.93
  16.1 0.8 iota_reduce_fusion.1
  17.0 0.7 fusion.185
  18.9 0.6 fusion.184
  48.0 4.5 broadcast_multiply_fusion
  52.5 40.2 %all-gather.5.cloned.1.call-done = bf16[8,1024,256]{2,1,0:T(8,128)(2,1)} async-done(((bf16[1,1024,256]{2,1,0:T(8,128)(2,1)}), bf16[8,1024,256]{2,1,0:T(8,128)(2,1)}) %all-gather.5.cloned.1.call-update) | async-done | bytes 4194320 | tf_op jit(solution)/shard_map/all_gather | solution.py:38
  92.8 1.9 fusion.79
  94.9 0.5 copy-done
  95.3 1.7 fusion.75
  98.3 0.4 fusion.69
  98.8 0.5 fusion.67
  100.3 3.1 copy.86
  103.4 8.3 %all-to-all-start = ((f32[4,32,16,256]{3,0,2,1:T(4,128)}), f32[4,32,16,256]{3,0,2,1:T(4,128)S(1)}, u32[]{:S(2)}, u32[]{:S(2)}) async-start(f32[4,32,16,256]{3,0,2,1:T(4,128)} %copy.86), calls=%async_computation | async-start | bytes 4194304 | tf_op jit(solution)/shard_map/all_to_all | solution.py:46
  111.9 1.0 copy.97
  112.9 71.9 %all-gather.7.cloned.1.call-done = bf16[8,1024,256]{2,1,0:T(8,128)(2,1)} async-done(((bf16[1,1024,256]{2,1,0:T(8,128)(2,1)}), bf16[8,1024,256]{2,1,0:T(8,128)(2,1)}) %all-gather.7.cloned.1.call-update) | async-done | bytes 4194320 | tf_op jit(solution)/shard_map/all_gather | solution.py:38
  185.0 1.9 fusion.78
  187.0 0.5 copy-done.1
  187.5 1.7 fusion.61
  191.0 0.5 fusion.53
  192.4 3.1 copy.90
  195.5 7.1 %all-to-all-start.1 = ((f32[4,32,16,256]{3,0,2,1:T(4,128)}), f32[4,32,16,256]{3,0,2,1:T(4,128)}, u32[]{:S(2)}, u32[]{:S(2)}) async-start(f32[4,32,16,256]{3,0,2,1:T(4,128)} %copy.90), calls=%async_computation.1 | async-start | bytes 4194304 | tf_op jit(solution)/shard_map/all_to_all | solution.py:46
  202.7 74.6 %all-gather.9.cloned.1.call-done = bf16[8,1024,256]{2,1,0:T(8,128)(2,1)} async-done(((bf16[1,1024,256]{2,1,0:T(8,128)(2,1)}), bf16[8,1024,256]{2,1,0:T(8,128)(2,1)}) %all-gather.9.cloned.1.call-update) | async-done | bytes 4194320 | tf_op jit(solution)/shard_map/all_gather | solution.py:38
  277.4 2.0 fusion.77
  279.4 0.5 copy-done.2
  279.9 1.7 fusion.47
  282.4 0.5 fusion.43
  284.4 0.5 fusion.35
  284.9 3.1 copy.94
  288.0 6.9 %all-to-all-start.2 = ((f32[4,32,16,256]{3,0,2,1:T(4,128)}), f32[4,32,16,256]{3,0,2,1:T(4,128)}, u32[]{:S(2)}, u32[]{:S(2)}) async-start(f32[4,32,16,256]{3,0,2,1:T(4,128)} %copy.94), calls=%async_computation.2 | async-start | bytes 4194304 | tf_op jit(solution)/shard_map/all_to_all | solution.py:46
  294.9 73.4 %all-gather.11.cloned.1.call-done = bf16[8,1024,256]{2,1,0:T(8,128)(2,1)} async-done(((bf16[1,1024,256]{2,1,0:T(8,128)(2,1)}), bf16[8,1024,256]{2,1,0:T(8,128)(2,1)}) %all-gather.11.cloned.1.call-update) | async-done | bytes 4194320 | tf_op jit(solution)/shard_map/all_gather | solution.py:38
  368.5 2.0 fusion.76
  370.5 0.5 copy-done.3
  371.0 1.7 fusion.33
  373.4 0.5 fusion.29
  375.4 0.5 fusion.21
  375.9 3.1 copy.98
  379.0 6.8 %all-to-all-start.3 = ((f32[4,32,16,256]{3,0,2,1:T(4,128)}), f32[4,32,16,256]{3,0,2,1:T(4,128)}, u32[]{:S(2)}, u32[]{:S(2)}) async-start(f32[4,32,16,256]{3,0,2,1:T(4,128)} %copy.98), calls=%async_computation.3 | async-start | bytes 4194304 | tf_op jit(solution)/shard_map/all_to_all | solution.py:46
  385.8 0.6 iota_reduce_fusion
  386.8 2.1 fusion.8
  389.1 3.5 fusion.11
  392.9 3.5 fusion.14
  396.8 39.2 %all-to-all-done.3 = f32[4,32,16,256]{3,0,2,1:T(4,128)} async-done(((f32[4,32,16,256]{3,0,2,1:T(4,128)}), f32[4,32,16,256]{3,0,2,1:T(4,128)}, u32[]{:S(2)}, u32[]{:S(2)}) %all-to-all-start.3) | async-done | bytes 2097184 | tf_op jit(solution)/shard_map/all_to_all | solution.py:46
  436.0 3.7 fusion.17
  439.9 2.5 maximum_add_fusion
  (95 shorter events, 12.6 us)
Async XLA Ops:
  6.5 86.1 %all-gather.5.cloned.1.call-start = ((), (), s32[]{:S(2)}) async-start(), calls=%async_computation.4 | async-start | bytes 4718592 | tf_op jit(solution)/shard_map/all_gather | solution.py:38
  12.7 3.2 copy-start.9
  12.7 3.2 copy-start.10
  12.7 25.3 %copy-start.11 = (s32[4,32]{1,0:T(4,128)S(1)}, s32[4,32]{1,0:T(4,128)}, u32[]{:S(2)}) copy-start(s32[4,32]{1,0:T(4,128)} %param.7) | copy-start | bytes 1540
  12.7 172.2 %all-gather.7.cloned.1.call-start = ((), (), s32[]{:S(2)}) async-start(), calls=%async_computation.5 | async-start | bytes 4718592 | tf_op jit(solution)/shard_map/all_gather | solution.py:38
  14.8 262.4 %all-gather.9.cloned.1.call-start = ((), (), s32[]{:S(2)}) async-start(), calls=%async_computation.6 | async-start | bytes 4718592 | tf_op jit(solution)/shard_map/all_gather | solution.py:38
  92.7 2.7 copy-start
  94.8 2.5 copy-start.7
  103.4 92.2 %all-to-all-start = ((f32[4,32,16,256]{3,0,2,1:T(4,128)}), f32[4,32,16,256]{3,0,2,1:T(4,128)S(1)}, u32[]{:S(2)}, u32[]{:S(2)}) async-start(f32[4,32,16,256]{3,0,2,1:T(4,128)} %copy.86), calls=%async_computation | async-start | bytes 4194304 | tf_op jit(solution)/shard_map/all_to_all | solution.py:46
  111.7 256.6 %all-gather.11.cloned.1.call-start = ((), (), s32[]{:S(2)}) async-start(), calls=%async_computation.7 | async-start | bytes 4718592 | tf_op jit(solution)/shard_map/all_gather | solution.py:38
  184.8 2.7 copy-start.1
  187.0 2.5 copy-start.6
  195.5 92.4 %all-to-all-start.1 = ((f32[4,32,16,256]{3,0,2,1:T(4,128)}), f32[4,32,16,256]{3,0,2,1:T(4,128)}, u32[]{:S(2)}, u32[]{:S(2)}) async-start(f32[4,32,16,256]{3,0,2,1:T(4,128)} %copy.90), calls=%async_computation.1 | async-start | bytes 4194304 | tf_op jit(solution)/shard_map/all_to_all | solution.py:46
  277.3 2.7 copy-start.2
  279.4 2.5 copy-start.5
  288.0 91.0 %all-to-all-start.2 = ((f32[4,32,16,256]{3,0,2,1:T(4,128)}), f32[4,32,16,256]{3,0,2,1:T(4,128)}, u32[]{:S(2)}, u32[]{:S(2)}) async-start(f32[4,32,16,256]{3,0,2,1:T(4,128)} %copy.94), calls=%async_computation.2 | async-start | bytes 4194304 | tf_op jit(solution)/shard_map/all_to_all | solution.py:46
  368.3 2.7 copy-start.3
  370.4 2.5 copy-start.8
  379.0 57.0 %all-to-all-start.3 = ((f32[4,32,16,256]{3,0,2,1:T(4,128)}), f32[4,32,16,256]{3,0,2,1:T(4,128)}, u32[]{:S(2)}, u32[]{:S(2)}) async-start(f32[4,32,16,256]{3,0,2,1:T(4,128)} %copy.98), calls=%async_computation.3 | async-start | bytes 4194304 | tf_op jit(solution)/shard_map/all_to_all | solution.py:46
  436.0 4.0 copy-start.4
Sparse Core Ops, SparseCore 0:
  12.8 79.8 all-gather.4
  95.3 89.4 all-gather.6
  187.5 89.7 all-gather.8
  279.8 88.4 all-gather.10

commit v4 on v3

--- a/solution.py
+++ b/solution.py
@@ -1,6 +1,10 @@
+import functools
+
 import jax
 import jax.numpy as jnp
 from jax import lax
+from jax.experimental import pallas as pl
+from jax.experimental.pallas import tpu as pltpu
 from jax.sharding import PartitionSpec as P
 
 SLOTS = 4
@@ -15,6 +19,58 @@
     is_first = first == order
     earlier = order[None, :] < first[:, None]
     return jnp.sum(earlier & is_first[None, :], axis=1).astype(jnp.int32)
+
+
+def gather_kernel(count, source, gathered, send_sems, recv_sems, local_sem):
+    me = lax.axis_index("blk")
+    column = lax.axis_index("grp")
+    local = pltpu.make_async_copy(source, gathered.at[me], local_sem)
+    local.start()
+    outgoing = []
+    for step in range(1, count):
+        peer = lax.rem(me + step, count)
+        copy = pltpu.make_async_remote_copy(
+            src_ref=source,
+            dst_ref=gathered.at[me],
+            send_sem=send_sems.at[step],
+            recv_sem=recv_sems.at[step],
+            device_id=(peer, column),
+            device_id_type=pl.DeviceIdType.MESH,
+        )
+        copy.start()
+        outgoing.append(copy)
+    for step in range(1, count):
+        sender = lax.rem(me + count - step, count)
+        incoming = pltpu.make_async_remote_copy(
+            src_ref=source,
+            dst_ref=gathered.at[sender],
+            send_sem=send_sems.at[step],
+            recv_sem=recv_sems.at[step],
+            device_id=(sender, column),
+            device_id_type=pl.DeviceIdType.MESH,
+        )
+        incoming.wait_recv()
+    for copy in outgoing:
+        copy.wait_send()
+    local.wait()
+
+
+def gather_blk(piece):
+    count = lax.axis_size("blk")
+    rows, width = piece.shape
+    return pl.pallas_call(
+        functools.partial(gather_kernel, count),
+        out_shape=jax.ShapeDtypeStruct((count, rows, width), piece.dtype),
+        in_specs=[pl.BlockSpec(memory_space=pl.ANY)],
+        out_specs=pl.BlockSpec(memory_space=pl.ANY),
+        scratch_shapes=[
+            pltpu.SemaphoreType.DMA((count,)),
+            pltpu.SemaphoreType.DMA((count,)),
+            pltpu.SemaphoreType.DMA(()),
+        ],
+        compiler_params=pltpu.CompilerParams(has_side_effects=True),
+        cost_estimate=pl.CostEstimate(flops=0, bytes_accessed=2 * count * rows * width * 2, transcendentals=0),
+    )(piece)
 
 
 def shards(amplitudes, pair_screen, integrals, tile_ab, tile_cd, residual_in):
@@ -35,7 +91,7 @@
     chunked = jnp.transpose(integrals.reshape(integrals.shape[1], CHUNKS, chunk), (1, 0, 2))
     pieces = []
     for part in range(CHUNKS):
-        portion = lax.all_gather(chunked[part : part + 1], "blk", axis=0, tiled=True)
+        portion = gather_blk(chunked[part])
         running = jnp.zeros((SLOTS, group_rows, chunk), jnp.float32)
         for offset in range(portion.shape[0]):
             rows_in = lax.dynamic_index_in_dim(masked, column_cd[offset], 0, keepdims=False)

time: 450 us -> 531 us (1.18)
  the two profiles are of different devices: /device:TPU:1 before, /device:TPU:27 now
where the time goes in v4:
time: 531 us; the launch traced here: 530 us
  Pallas kernels  336 us (63%)
  matrix products  46.3 us (9%)
  starting transfers between devices  41.2 us (8%)
  waiting for transfers between devices  39.2 us (7%)
  between operations  30.5 us (6%)
  local copies, waits for them, and re-layouts  27.9 us (5%)
  other arithmetic  9.5 us (2%)
    pallas_call x4, Pallas kernels, gather_blk(): pl.pallas_call(functools.partial(gather_kernel, count), out_shape=jax.Sha...  336 us
    all_to_all x4, starting transfers between devices, shards(): lax.all_to_all(running.reshape(SLOTS, grp_count, owner_rows, chunk), 'grp...  41.2 us
    all_to_all x4, waiting for transfers between devices, shards(): lax.all_to_all(running.reshape(SLOTS, grp_count, owner_rows, chunk), 'grp...  39.2 us
    dot_general x32, matrix products, shards(): jnp.dot(rows_in, portion[offset], preferred_element_type=jnp.float32)  33.4 us
    dot_general x4, matrix products, shards(): jnp.einsum('nsg,sgrc->rnc', onehot, arrived, precision=lax.Precision.HIGH...  12.8 us
    reshape x4, local copies, waits for them, and re-layouts, shards(): running.reshape(SLOTS, grp_count, owner_rows, chunk)  12.5 us
  transfers between devices with their start and end apart: 4, of which 1 were waited for; matrix products, arithmetic and copies ran while one was open for 8% of the time, Pallas kernels for 48%

profile of v4, /device:TPU:27, one launch (start us, length us, event | category | flops | bytes accessed | tf_op | source)
XLA Modules:
  0.0 530.1 jit_solution(2624452702784996582)
XLA Ops:
  0.0 0.9 constant_dynamic-slice_fusion.29
  0.9 0.7 iota_reduce_fusion.1
  1.8 0.7 fusion.248
  3.8 0.6 fusion.247
  22.9 0.7 convert_element_type.18
  23.8 3.9 copy.41
  27.7 2.8 copy.42
  30.6 1.4 slice_bitcast_fusion.3
  31.9 79.2 %shard_map.64 = bf16[8,1024,256]{2,1,0:T(8,128)(2,1)} custom-call(bf16[1024,256]{1,0:T(8,128)(2,1)} %get-tuple-element.9.source), custom_call_target="tpu_custom_call" | custom-call | bytes 8388608 | tf_op jit(solution)/shard_map/pallas_call | solution.py:61
  112.4 4.5 broadcast_multiply_fusion
  117.6 1.8 fusion.79
  120.1 1.8 fusion.75
  123.3 1.8 fusion.73
  126.3 1.8 fusion.71
  129.4 1.8 fusion.69
  132.5 1.8 fusion.67
  135.6 1.8 fusion.65
  138.7 1.8 fusion.63
  140.5 3.2 copy.43
  143.7 10.2 %all-to-all-start = ((f32[4,32,16,256]{3,0,2,1:T(4,128)}), f32[4,32,16,256]{3,0,2,1:T(4,128)S(1)}, u32[]{:S(2)}, u32[]{:S(2)}) async-start(f32[4,32,16,256]{3,0,2,1:T(4,128)} %copy.43), calls=%async_computation | async-start | bytes 4194304 | tf_op jit(solution)/shard_map/all_to_all | solution.py:102
  153.9 85.8 %shard_map.65 = bf16[8,1024,256]{2,1,0:T(8,128)(2,1)} custom-call(bf16[1024,256]{1,0:T(8,128)(2,1)} %get-tuple-element.12.source), custom_call_target="tpu_custom_call" | custom-call | bytes 8388608 | tf_op jit(solution)/shard_map/pallas_call | solution.py:61
  239.9 2.0 fusion.78
  241.9 0.5 copy-done
  242.3 1.7 fusion.61
  245.8 0.5 fusion.53
  246.3 0.5 fusion.51
  246.8 0.5 fusion.49
  247.3 3.1 copy.46
  250.4 9.7 %all-to-all-start.1 = ((f32[4,32,16,256]{3,0,2,1:T(4,128)}), f32[4,32,16,256]{3,0,2,1:T(4,128)}, u32[]{:S(2)}, u32[]{:S(2)}) async-start(f32[4,32,16,256]{3,0,2,1:T(4,128)} %copy.46), calls=%async_computation.1 | async-start | bytes 4194304 | tf_op jit(solution)/shard_map/all_to_all | solution.py:102
  260.1 86.0 %shard_map.66 = bf16[8,1024,256]{2,1,0:T(8,128)(2,1)} custom-call(bf16[1024,256]{1,0:T(8,128)(2,1)} %get-tuple-element.11.source), custom_call_target="tpu_custom_call" | custom-call | bytes 8388608 | tf_op jit(solution)/shard_map/pallas_call | solution.py:61
  346.4 1.9 fusion.77
  348.4 0.5 copy-done.1
  348.8 1.7 fusion.47
  353.8 3.1 copy.49
  356.9 10.2 %all-to-all-start.2 = ((f32[4,32,16,256]{3,0,2,1:T(4,128)}), f32[4,32,16,256]{3,0,2,1:T(4,128)}, u32[]{:S(2)}, u32[]{:S(2)}) async-start(f32[4,32,16,256]{3,0,2,1:T(4,128)} %copy.49), calls=%async_computation.2 | async-start | bytes 4194304 | tf_op jit(solution)/shard_map/all_to_all | solution.py:102
  367.2 84.5 %shard_map.67 = bf16[8,1024,256]{2,1,0:T(8,128)(2,1)} custom-call(bf16[1024,256]{1,0:T(8,128)(2,1)} %get-tuple-element.10.source), custom_call_target="tpu_custom_call" | custom-call | bytes 8388608 | tf_op jit(solution)/shard_map/pallas_call | solution.py:61
  451.8 1.9 fusion.76
  453.9 0.5 copy-done.2
  454.3 1.7 fusion.33
  459.3 3.1 copy.52
  462.4 11.0 %all-to-all-start.3 = ((f32[4,32,16,256]{3,0,2,1:T(4,128)}), f32[4,32,16,256]{3,0,2,1:T(4,128)}, u32[]{:S(2)}, u32[]{:S(2)}) async-start(f32[4,32,16,256]{3,0,2,1:T(4,128)} %copy.52), calls=%async_computation.3 | async-start | bytes 4194304 | tf_op jit(solution)/shard_map/all_to_all | solution.py:102
  473.4 0.6 iota_reduce_fusion
  474.4 2.1 fusion.8
  476.7 3.5 fusion.11
  480.6 3.5 fusion.14
  484.4 39.2 %all-to-all-done.3 = f32[4,32,16,256]{3,0,2,1:T(4,128)} async-done(((f32[4,32,16,256]{3,0,2,1:T(4,128)}), f32[4,32,16,256]{3,0,2,1:T(4,128)}, u32[]{:S(2)}, u32[]{:S(2)}) %all-to-all-start.3) | async-done | bytes 2097184 | tf_op jit(solution)/shard_map/all_to_all | solution.py:102
  523.6 3.7 fusion.17
  527.6 2.5 maximum_add_fusion
  (76 shorter events, 10.9 us)
Async XLA Ops:
  143.7 106.7 %all-to-all-start = ((f32[4,32,16,256]{3,0,2,1:T(4,128)}), f32[4,32,16,256]{3,0,2,1:T(4,128)S(1)}, u32[]{:S(2)}, u32[]{:S(2)}) async-start(f32[4,32,16,256]{3,0,2,1:T(4,128)} %copy.43), calls=%async_computation | async-start | bytes 4194304 | tf_op jit(solution)/shard_map/all_to_all | solution.py:102
  239.7 2.7 copy-start
  241.8 2.5 copy-start.4
  250.4 106.5 %all-to-all-start.1 = ((f32[4,32,16,256]{3,0,2,1:T(4,128)}), f32[4,32,16,256]{3,0,2,1:T(4,128)}, u32[]{:S(2)}, u32[]{:S(2)}) async-start(f32[4,32,16,256]{3,0,2,1:T(4,128)} %copy.46), calls=%async_computation.1 | async-start | bytes 4194304 | tf_op jit(solution)/shard_map/all_to_all | solution.py:102
  346.2 2.7 copy-start.1
  348.3 2.5 copy-start.5
  356.9 105.4 %all-to-all-start.2 = ((f32[4,32,16,256]{3,0,2,1:T(4,128)}), f32[4,32,16,256]{3,0,2,1:T(4,128)}, u32[]{:S(2)}, u32[]{:S(2)}) async-start(f32[4,32,16,256]{3,0,2,1:T(4,128)} %copy.49), calls=%async_computation.2 | async-start | bytes 4194304 | tf_op jit(solution)/shard_map/all_to_all | solution.py:102
  451.7 2.7 copy-start.2
  453.8 2.5 copy-start.3
  462.4 11.0 %copy-start.7 = (s32[8,32]{1,0:T(8,128)S(1)}, s32[8,32]{1,0:T(8,128)}, u32[]{:S(2)}) copy-start(s32[8,32]{1,0:T(8,128)} %param.9) | copy-start | bytes 3076
  462.4 61.2 %all-to-all-start.3 = ((f32[4,32,16,256]{3,0,2,1:T(4,128)}), f32[4,32,16,256]{3,0,2,1:T(4,128)}, u32[]{:S(2)}, u32[]{:S(2)}) async-start(f32[4,32,16,256]{3,0,2,1:T(4,128)} %copy.52), calls=%async_computation.3 | async-start | bytes 4194304 | tf_op jit(solution)/shard_map/all_to_all | solution.py:102
  523.6 4.0 copy-start.6

commit v5 on v4

--- a/solution.py
+++ b/solution.py
@@ -24,33 +24,36 @@
 def gather_kernel(count, source, gathered, send_sems, recv_sems, local_sem):
     me = lax.axis_index("blk")
     column = lax.axis_index("grp")
+    ring = count // 2
+    base = (me // ring) * ring
+    partner = lax.rem(me + ring, count)
     local = pltpu.make_async_copy(source, gathered.at[me], local_sem)
     local.start()
-    outgoing = []
-    for step in range(1, count):
-        peer = lax.rem(me + step, count)
-        copy = pltpu.make_async_remote_copy(
-            src_ref=source,
-            dst_ref=gathered.at[me],
-            send_sem=send_sems.at[step],
-            recv_sem=recv_sems.at[step],
-            device_id=(peer, column),
+
+    def transfer(origin, target, slot):
+        return pltpu.make_async_remote_copy(
+            src_ref=source if origin is me else gathered.at[origin],
+            dst_ref=gathered.at[origin],
+            send_sem=send_sems.at[slot],
+            recv_sem=recv_sems.at[origin],
+            device_id=(target, column),
             device_id_type=pl.DeviceIdType.MESH,
         )
+
+    peers = [base + lax.rem(me - base + step, ring) for step in range(1, ring)]
+    outgoing = [transfer(me, partner, 0)]
+    for step, peer in enumerate(peers):
+        outgoing.append(transfer(me, peer, 1 + step))
+    for copy in outgoing:
         copy.start()
-        outgoing.append(copy)
-    for step in range(1, count):
-        sender = lax.rem(me + count - step, count)
-        incoming = pltpu.make_async_remote_copy(
-            src_ref=source,
-            dst_ref=gathered.at[sender],
-            send_sem=send_sems.at[step],
-            recv_sem=recv_sems.at[step],
-            device_id=(sender, column),
-            device_id_type=pl.DeviceIdType.MESH,
-        )
-        incoming.wait_recv()
-    for copy in outgoing:
+    transfer(partner, partner, 0).wait_recv()
+    forwarded = [transfer(partner, peer, ring + step) for step, peer in enumerate(peers)]
+    for copy in forwarded:
+        copy.start()
+    for peer in peers:
+        transfer(peer, peer, 0).wait_recv()
+        transfer(lax.rem(peer + ring, count), peer, 0).wait_recv()
+    for copy in outgoing + forwarded:
         copy.wait_send()
     local.wait()
 

time: 531 us -> 431 us (0.81)
  the two profiles are of different devices: /device:TPU:27 before, /device:TPU:1 now
where the time goes in v5:
time: 431 us; the launch traced here: 430 us
  Pallas kernels  237 us (55%)
  matrix products  46.3 us (11%)
  starting transfers between devices  39.2 us (9%)
  waiting for transfers between devices  39.1 us (9%)
  between operations  30.5 us (7%)
  local copies, waits for them, and re-layouts  27.9 us (6%)
  other arithmetic  9.5 us (2%)
    pallas_call x4, Pallas kernels, gather_blk(): pl.pallas_call(functools.partial(gather_kernel, count), out_shape=jax.Sha...  237 us
    all_to_all x4, starting transfers between devices, shards(): lax.all_to_all(running.reshape(SLOTS, grp_count, owner_rows, chunk), 'grp...  39.2 us
    all_to_all x4, waiting for transfers between devices, shards(): lax.all_to_all(running.reshape(SLOTS, grp_count, owner_rows, chunk), 'grp...  39.1 us
    dot_general x32, matrix products, shards(): jnp.dot(rows_in, portion[offset], preferred_element_type=jnp.float32)  33.5 us
    dot_general x4, matrix products, shards(): jnp.einsum('nsg,sgrc->rnc', onehot, arrived, precision=lax.Precision.HIGH...  12.8 us
    reshape x4, local copies, waits for them, and re-layouts, shards(): running.reshape(SLOTS, grp_count, owner_rows, chunk)  12.5 us
  transfers between devices with their start and end apart: 4, of which 1 were waited for; matrix products, arithmetic and copies ran while one was open for 9% of the time, Pallas kernels for 41%

profile of v5, /device:TPU:1, one launch (start us, length us, event | category | flops | bytes accessed | tf_op | source)
XLA Modules:
  0.0 429.7 jit_solution(12699903659277907133)
XLA Ops:
  0.0 0.9 constant_dynamic-slice_fusion.29
  0.9 0.7 iota_reduce_fusion.1
  1.8 0.7 fusion.248
  3.8 0.6 fusion.247
  22.9 0.7 convert_element_type.18
  23.8 3.9 copy.41
  27.7 2.8 copy.42
  30.6 1.4 slice_bitcast_fusion.3
  31.9 62.9 %shard_map.64 = bf16[8,1024,256]{2,1,0:T(8,128)(2,1)} custom-call(bf16[1024,256]{1,0:T(8,128)(2,1)} %get-tuple-element.9.source), custom_call_target="tpu_custom_call" | custom-call | bytes 8388608 | tf_op jit(solution)/shard_map/pallas_call | solution.py:64
  96.1 4.5 %broadcast_multiply_fusion = bf16[4,512,1024]{2,1,0:T(8,128)(2,1)} fusion(bf16[4,512,1024]{2,1,0:T(8,128)(2,1)} %param.6, bf16[4,512]{1,0:T(4,128)(2,1)S(1)} %convert_element_type.19), kind=kLoop, calls=%fused_computation.9 | loop fusion | flops 2097152 | bytes 8392704 | tf_op jit(solution)/shard_map/mul | solution.py:85
  101.4 1.8 fusion.79
  103.8 1.8 fusion.75
  107.1 1.8 fusion.73
  110.0 1.8 fusion.71
  113.1 1.8 fusion.69
  116.3 1.8 fusion.67
  119.4 1.8 fusion.65
  122.4 1.8 fusion.63
  124.2 3.2 copy.43
  127.4 9.6 %all-to-all-start = ((f32[4,32,16,256]{3,0,2,1:T(4,128)}), f32[4,32,16,256]{3,0,2,1:T(4,128)S(1)}, u32[]{:S(2)}, u32[]{:S(2)}) async-start(f32[4,32,16,256]{3,0,2,1:T(4,128)} %copy.43), calls=%async_computation | async-start | bytes 4194304 | tf_op jit(solution)/shard_map/all_to_all | solution.py:105
  137.1 58.1 %shard_map.65 = bf16[8,1024,256]{2,1,0:T(8,128)(2,1)} custom-call(bf16[1024,256]{1,0:T(8,128)(2,1)} %get-tuple-element.12.source), custom_call_target="tpu_custom_call" | custom-call | bytes 8388608 | tf_op jit(solution)/shard_map/pallas_call | solution.py:64
  195.4 1.9 fusion.78
  197.4 0.5 copy-done
  197.9 1.7 fusion.61
  201.3 0.5 fusion.53
  202.4 0.5 fusion.49
  202.8 3.1 copy.46
  205.9 9.8 %all-to-all-start.1 = ((f32[4,32,16,256]{3,0,2,1:T(4,128)}), f32[4,32,16,256]{3,0,2,1:T(4,128)}, u32[]{:S(2)}, u32[]{:S(2)}) async-start(f32[4,32,16,256]{3,0,2,1:T(4,128)} %copy.46), calls=%async_computation.1 | async-start | bytes 4194304 | tf_op jit(solution)/shard_map/all_to_all | solution.py:105
  215.7 58.0 %shard_map.66 = bf16[8,1024,256]{2,1,0:T(8,128)(2,1)} custom-call(bf16[1024,256]{1,0:T(8,128)(2,1)} %get-tuple-element.11.source), custom_call_target="tpu_custom_call" | custom-call | bytes 8388608 | tf_op jit(solution)/shard_map/pallas_call | solution.py:64
  274.0 2.0 fusion.77
  276.0 0.5 copy-done.1
  276.5 1.7 fusion.47
  280.4 0.5 fusion.37
  281.4 3.1 copy.49
  284.6 9.8 %all-to-all-start.2 = ((f32[4,32,16,256]{3,0,2,1:T(4,128)}), f32[4,32,16,256]{3,0,2,1:T(4,128)}, u32[]{:S(2)}, u32[]{:S(2)}) async-start(f32[4,32,16,256]{3,0,2,1:T(4,128)} %copy.49), calls=%async_computation.2 | async-start | bytes 4194304 | tf_op jit(solution)/shard_map/all_to_all | solution.py:105
  294.4 58.0 %shard_map.67 = bf16[8,1024,256]{2,1,0:T(8,128)(2,1)} custom-call(bf16[1024,256]{1,0:T(8,128)(2,1)} %get-tuple-element.10.source), custom_call_target="tpu_custom_call" | custom-call | bytes 8388608 | tf_op jit(solution)/shard_map/pallas_call | solution.py:64
  352.6 1.9 fusion.76
  354.6 0.5 copy-done.2
  355.1 1.7 fusion.33
  360.0 3.1 copy.52
  363.1 9.9 %all-to-all-start.3 = ((f32[4,32,16,256]{3,0,2,1:T(4,128)}), f32[4,32,16,256]{3,0,2,1:T(4,128)}, u32[]{:S(2)}, u32[]{:S(2)}) async-start(f32[4,32,16,256]{3,0,2,1:T(4,128)} %copy.52), calls=%async_computation.3 | async-start | bytes 4194304 | tf_op jit(solution)/shard_map/all_to_all | solution.py:105
  373.1 0.6 iota_reduce_fusion
  374.1 2.1 fusion.8
  376.4 3.5 fusion.11
  380.2 3.5 fusion.14
  384.1 39.1 %all-to-all-done.3 = f32[4,32,16,256]{3,0,2,1:T(4,128)} async-done(((f32[4,32,16,256]{3,0,2,1:T(4,128)}), f32[4,32,16,256]{3,0,2,1:T(4,128)}, u32[]{:S(2)}, u32[]{:S(2)}) %all-to-all-start.3) | async-done | bytes 2097184 | tf_op jit(solution)/shard_map/all_to_all | solution.py:105
  423.2 3.7 fusion.17
  427.2 2.5 maximum_add_fusion
  (76 shorter events, 11.0 us)
Async XLA Ops:
  127.4 78.5 %all-to-all-start = ((f32[4,32,16,256]{3,0,2,1:T(4,128)}), f32[4,32,16,256]{3,0,2,1:T(4,128)S(1)}, u32[]{:S(2)}, u32[]{:S(2)}) async-start(f32[4,32,16,256]{3,0,2,1:T(4,128)} %copy.43), calls=%async_computation | async-start | bytes 4194304 | tf_op jit(solution)/shard_map/all_to_all | solution.py:105
  195.2 2.7 copy-start
  197.3 2.5 copy-start.4
  205.9 78.6 %all-to-all-start.1 = ((f32[4,32,16,256]{3,0,2,1:T(4,128)}), f32[4,32,16,256]{3,0,2,1:T(4,128)}, u32[]{:S(2)}, u32[]{:S(2)}) async-start(f32[4,32,16,256]{3,0,2,1:T(4,128)} %copy.46), calls=%async_computation.1 | async-start | bytes 4194304 | tf_op jit(solution)/shard_map/all_to_all | solution.py:105
  273.8 2.7 copy-start.1
  275.9 2.5 copy-start.5
  284.6 78.6 %all-to-all-start.2 = ((f32[4,32,16,256]{3,0,2,1:T(4,128)}), f32[4,32,16,256]{3,0,2,1:T(4,128)}, u32[]{:S(2)}, u32[]{:S(2)}) async-start(f32[4,32,16,256]{3,0,2,1:T(4,128)} %copy.49), calls=%async_computation.2 | async-start | bytes 4194304 | tf_op jit(solution)/shard_map/all_to_all | solution.py:105
  352.4 2.7 copy-start.2
  354.6 2.5 copy-start.3
  363.1 9.9 %copy-start.7 = (s32[8,32]{1,0:T(8,128)S(1)}, s32[8,32]{1,0:T(8,128)}, u32[]{:S(2)}) copy-start(s32[8,32]{1,0:T(8,128)} %param.9) | copy-start | bytes 3076
  363.1 60.0 %all-to-all-start.3 = ((f32[4,32,16,256]{3,0,2,1:T(4,128)}), f32[4,32,16,256]{3,0,2,1:T(4,128)}, u32[]{:S(2)}, u32[]{:S(2)}) async-start(f32[4,32,16,256]{3,0,2,1:T(4,128)} %copy.52), calls=%async_computation.3 | async-start | bytes 4194304 | tf_op jit(solution)/shard_map/all_to_all | solution.py:105
  423.2 4.0 copy-start.6

commit v6 on v5

--- a/solution.py
+++ b/solution.py
@@ -26,34 +26,53 @@
     column = lax.axis_index("grp")
     ring = count // 2
     base = (me // ring) * ring
-    partner = lax.rem(me + ring, count)
+    half = source.shape[0] // 2
+    pieces = (pl.ds(0, half), pl.ds(half, half))
+
+    def along(step):
+        return base + lax.rem(me - base + step + ring, ring)
+
+    def across(device):
+        return lax.rem(device + ring, count)
+
+    partner, right, left, opposite = across(me), along(1), along(-1), along(2)
     local = pltpu.make_async_copy(source, gathered.at[me], local_sem)
     local.start()
 
-    def transfer(origin, target, slot):
+    def transfer(origin, target, slot, piece=None):
+        src = source if origin is me else gathered.at[origin]
+        dst = gathered.at[origin]
+        if piece is not None:
+            src, dst = src.at[pieces[piece]], dst.at[pieces[piece]]
         return pltpu.make_async_remote_copy(
-            src_ref=source if origin is me else gathered.at[origin],
-            dst_ref=gathered.at[origin],
+            src_ref=src,
+            dst_ref=dst,
             send_sem=send_sems.at[slot],
-            recv_sem=recv_sems.at[origin],
+            recv_sem=recv_sems.at[origin, 0 if piece is None else piece],
             device_id=(target, column),
             device_id_type=pl.DeviceIdType.MESH,
         )
 
-    peers = [base + lax.rem(me - base + step, ring) for step in range(1, ring)]
-    outgoing = [transfer(me, partner, 0)]
-    for step, peer in enumerate(peers):
-        outgoing.append(transfer(me, peer, 1 + step))
-    for copy in outgoing:
+    sent = [transfer(me, partner, 0), transfer(me, right, 1), transfer(me, left, 2)]
+    for copy in sent:
         copy.start()
-    transfer(partner, partner, 0).wait_recv()
-    forwarded = [transfer(partner, peer, ring + step) for step, peer in enumerate(peers)]
-    for copy in forwarded:
-        copy.start()
-    for peer in peers:
-        transfer(peer, peer, 0).wait_recv()
-        transfer(lax.rem(peer + ring, count), peer, 0).wait_recv()
-    for copy in outgoing + forwarded:
+    relays = [
+        (partner, partner, ((right, 3, None), (left, 4, None))),
+        (left, left, ((right, 5, 0),)),
+        (right, right, ((left, 6, 1),)),
+        (across(left), left, ((right, 7, 0),)),
+        (across(right), right, ((left, 8, 1),)),
+    ]
+    for origin, sender, onward in relays:
+        transfer(origin, sender, 0).wait_recv()
+        for target, slot, piece in onward:
+            copy = transfer(origin, target, slot, piece)
+            copy.start()
+            sent.append(copy)
+    for origin in (opposite, across(opposite)):
+        transfer(origin, left, 0, 0).wait_recv()
+        transfer(origin, right, 0, 1).wait_recv()
+    for copy in sent:
         copy.wait_send()
     local.wait()
 
@@ -67,8 +86,8 @@
         in_specs=[pl.BlockSpec(memory_space=pl.ANY)],
         out_specs=pl.BlockSpec(memory_space=pl.ANY),
         scratch_shapes=[
-            pltpu.SemaphoreType.DMA((count,)),
-            pltpu.SemaphoreType.DMA((count,)),
+            pltpu.SemaphoreType.DMA((count + 1,)),
+            pltpu.SemaphoreType.DMA((count, 2)),
             pltpu.SemaphoreType.DMA(()),
         ],
         compiler_params=pltpu.CompilerParams(has_side_effects=True),

time: 431 us -> 427 us (level); the launches traced: 430 us -> 420 us
  Pallas kernels: 237 us -> 224 us
    pallas_call x4, Pallas kernels: 237 us -> 224 us  [gather_blk(): pl.pallas_call(functools.partial(gather_kernel, count), out_shape=jax.Sha...]
  transfers between devices with their start and end apart: 4 -> 4, of which waited for: 1 -> 1; matrix products, arithmetic and copies ran while one was open for 9% -> 10% of each run, Pallas kernels for 41% -> 40%
where the time goes in v6:
time: 427 us; the launch traced here: 420 us
  Pallas kernels  224 us (52%)
  matrix products  46.3 us (11%)
  starting transfers between devices  42.4 us (10%)
  waiting for transfers between devices  39.1 us (9%)
  between operations  30.9 us (7%)
  local copies, waits for them, and re-layouts  27.9 us (7%)
  other arithmetic  9.5 us (2%)
    pallas_call x4, Pallas kernels, gather_blk(): pl.pallas_call(functools.partial(gather_kernel, count), out_shape=jax.Sha...  224 us
    all_to_all x4, starting transfers between devices, shards(): lax.all_to_all(running.reshape(SLOTS, grp_count, owner_rows, chunk), 'grp...  42.4 us
    all_to_all x4, waiting for transfers between devices, shards(): lax.all_to_all(running.reshape(SLOTS, grp_count, owner_rows, chunk), 'grp...  39.1 us
    dot_general x32, matrix products, shards(): jnp.dot(rows_in, portion[offset], preferred_element_type=jnp.float32)  33.4 us
    dot_general x4, matrix products, shards(): jnp.einsum('nsg,sgrc->rnc', onehot, arrived, precision=lax.Precision.HIGH...  12.8 us
    reshape x4, local copies, waits for them, and re-layouts, shards(): running.reshape(SLOTS, grp_count, owner_rows, chunk)  12.5 us
  transfers between devices with their start and end apart: 4, of which 1 were waited for; matrix products, arithmetic and copies ran while one was open for 10% of the time, Pallas kernels for 40%

profile of v6, /device:TPU:1, one launch (start us, length us, event | category | flops | bytes accessed | tf_op | source)
XLA Modules:
  0.0 420.0 jit_solution(5254251300749261131)
XLA Ops:
  0.0 0.9 constant_dynamic-slice_fusion.29
  0.9 0.7 iota_reduce_fusion.1
  1.8 0.7 fusion.248
  3.8 0.6 fusion.247
  22.9 0.7 convert_element_type.18
  23.8 3.9 copy.41
  27.7 2.8 copy.42
  30.6 1.4 slice_bitcast_fusion.3
  31.9 54.7 %shard_map.64 = bf16[8,1024,256]{2,1,0:T(8,128)(2,1)} custom-call(bf16[1024,256]{1,0:T(8,128)(2,1)} %get-tuple-element.9.source), custom_call_target="tpu_custom_call" | custom-call | bytes 8388608 | tf_op jit(solution)/shard_map/pallas_call | solution.py:83
  87.9 4.5 %broadcast_multiply_fusion = bf16[4,512,1024]{2,1,0:T(8,128)(2,1)} fusion(bf16[4,512,1024]{2,1,0:T(8,128)(2,1)} %param.6, bf16[4,512]{1,0:T(4,128)(2,1)S(1)} %convert_element_type.19), kind=kLoop, calls=%fused_computation.9 | loop fusion | flops 2097152 | bytes 8392704 | tf_op jit(solution)/shard_map/mul | solution.py:104
  93.1 1.8 fusion.79
  95.6 1.8 fusion.75
  98.8 1.8 fusion.73
  101.8 1.8 fusion.71
  104.9 1.8 fusion.69
  108.0 1.8 fusion.67
  111.1 1.8 fusion.65
  114.2 1.8 fusion.63
  116.0 3.2 copy.43
  119.2 9.3 %all-to-all-start = ((f32[4,32,16,256]{3,0,2,1:T(4,128)}), f32[4,32,16,256]{3,0,2,1:T(4,128)S(1)}, u32[]{:S(2)}, u32[]{:S(2)}) async-start(f32[4,32,16,256]{3,0,2,1:T(4,128)} %copy.43), calls=%async_computation | async-start | bytes 4194304 | tf_op jit(solution)/shard_map/all_to_all | solution.py:124
  128.5 56.7 %shard_map.65 = bf16[8,1024,256]{2,1,0:T(8,128)(2,1)} custom-call(bf16[1024,256]{1,0:T(8,128)(2,1)} %get-tuple-element.12.source), custom_call_target="tpu_custom_call" | custom-call | bytes 8388608 | tf_op jit(solution)/shard_map/pallas_call | solution.py:83
  185.4 1.9 fusion.78
  187.4 0.5 copy-done
  187.9 1.7 fusion.61
  192.8 3.1 copy.46
  195.9 10.4 %all-to-all-start.1 = ((f32[4,32,16,256]{3,0,2,1:T(4,128)}), f32[4,32,16,256]{3,0,2,1:T(4,128)}, u32[]{:S(2)}, u32[]{:S(2)}) async-start(f32[4,32,16,256]{3,0,2,1:T(4,128)} %copy.46), calls=%async_computation.1 | async-start | bytes 4194304 | tf_op jit(solution)/shard_map/all_to_all | solution.py:124
  206.3 56.0 %shard_map.66 = bf16[8,1024,256]{2,1,0:T(8,128)(2,1)} custom-call(bf16[1024,256]{1,0:T(8,128)(2,1)} %get-tuple-element.11.source), custom_call_target="tpu_custom_call" | custom-call | bytes 8388608 | tf_op jit(solution)/shard_map/pallas_call | solution.py:83
  262.5 1.9 fusion.77
  264.5 0.5 copy-done.1
  264.9 1.7 fusion.47
  269.9 3.1 copy.49
  273.0 12.1 %all-to-all-start.2 = ((f32[4,32,16,256]{3,0,2,1:T(4,128)}), f32[4,32,16,256]{3,0,2,1:T(4,128)}, u32[]{:S(2)}, u32[]{:S(2)}) async-start(f32[4,32,16,256]{3,0,2,1:T(4,128)} %copy.49), calls=%async_computation.2 | async-start | bytes 4194304 | tf_op jit(solution)/shard_map/all_to_all | solution.py:124
  285.1 56.5 %shard_map.67 = bf16[8,1024,256]{2,1,0:T(8,128)(2,1)} custom-call(bf16[1024,256]{1,0:T(8,128)(2,1)} %get-tuple-element.10.source), custom_call_target="tpu_custom_call" | custom-call | bytes 8388608 | tf_op jit(solution)/shard_map/pallas_call | solution.py:83
  341.8 2.0 fusion.76
  343.8 0.5 copy-done.2
  344.3 1.7 fusion.33
  347.7 0.5 fusion.25
  348.2 0.5 fusion.23
  348.7 0.5 fusion.21
  349.2 3.1 copy.52
  352.3 10.7 %all-to-all-start.3 = ((f32[4,32,16,256]{3,0,2,1:T(4,128)}), f32[4,32,16,256]{3,0,2,1:T(4,128)}, u32[]{:S(2)}, u32[]{:S(2)}) async-start(f32[4,32,16,256]{3,0,2,1:T(4,128)} %copy.52), calls=%async_computation.3 | async-start | bytes 4194304 | tf_op jit(solution)/shard_map/all_to_all | solution.py:124
  363.0 0.6 iota_reduce_fusion
  364.0 2.1 fusion.8
  366.3 3.5 fusion.11
  370.2 3.5 fusion.14
  374.0 39.1 %all-to-all-done.3 = f32[4,32,16,256]{3,0,2,1:T(4,128)} async-done(((f32[4,32,16,256]{3,0,2,1:T(4,128)}), f32[4,32,16,256]{3,0,2,1:T(4,128)}, u32[]{:S(2)}, u32[]{:S(2)}) %all-to-all-start.3) | async-done | bytes 2097184 | tf_op jit(solution)/shard_map/all_to_all | solution.py:124
  413.1 3.7 fusion.17
  417.1 2.5 maximum_add_fusion
  (76 shorter events, 10.9 us)
Async XLA Ops:
  119.2 76.7 %all-to-all-start = ((f32[4,32,16,256]{3,0,2,1:T(4,128)}), f32[4,32,16,256]{3,0,2,1:T(4,128)S(1)}, u32[]{:S(2)}, u32[]{:S(2)}) async-start(f32[4,32,16,256]{3,0,2,1:T(4,128)} %copy.43), calls=%async_computation | async-start | bytes 4194304 | tf_op jit(solution)/shard_map/all_to_all | solution.py:124
  185.2 2.7 copy-start
  187.3 2.5 copy-start.4
  195.9 77.1 %all-to-all-start.1 = ((f32[4,32,16,256]{3,0,2,1:T(4,128)}), f32[4,32,16,256]{3,0,2,1:T(4,128)}, u32[]{:S(2)}, u32[]{:S(2)}) async-start(f32[4,32,16,256]{3,0,2,1:T(4,128)} %copy.46), calls=%async_computation.1 | async-start | bytes 4194304 | tf_op jit(solution)/shard_map/all_to_all | solution.py:124
  262.3 2.7 copy-start.1
  264.4 2.5 copy-start.5
  273.0 79.3 %all-to-all-start.2 = ((f32[4,32,16,256]{3,0,2,1:T(4,128)}), f32[4,32,16,256]{3,0,2,1:T(4,128)}, u32[]{:S(2)}, u32[]{:S(2)}) async-start(f32[4,32,16,256]{3,0,2,1:T(4,128)} %copy.49), calls=%async_computation.2 | async-start | bytes 4194304 | tf_op jit(solution)/shard_map/all_to_all | solution.py:124
  341.6 2.7 copy-start.2
  343.7 2.5 copy-start.3
  352.3 10.7 %copy-start.7 = (s32[8,32]{1,0:T(8,128)S(1)}, s32[8,32]{1,0:T(8,128)}, u32[]{:S(2)}) copy-start(s32[8,32]{1,0:T(8,128)} %param.9) | copy-start | bytes 3076
  352.3 60.8 %all-to-all-start.3 = ((f32[4,32,16,256]{3,0,2,1:T(4,128)}), f32[4,32,16,256]{3,0,2,1:T(4,128)}, u32[]{:S(2)}, u32[]{:S(2)}) async-start(f32[4,32,16,256]{3,0,2,1:T(4,128)} %copy.52), calls=%async_computation.3 | async-start | bytes 4194304 | tf_op jit(solution)/shard_map/all_to_all | solution.py:124
  413.1 4.0 copy-start.6

commit v7 on v6

--- a/solution.py
+++ b/solution.py
@@ -111,10 +111,13 @@
     onehot = jnp.any(ab_hit[:, :, None, :] & slot_hit[None, :, :, :], axis=1).astype(jnp.float32)
     chunk = tile_width // CHUNKS
     chunked = jnp.transpose(integrals.reshape(integrals.shape[1], CHUNKS, chunk), (1, 0, 2))
+    halves = jnp.transpose(integrals.reshape(integrals.shape[1], 2, tile_width // 2), (1, 0, 2))
+    offloaded = lax.all_gather(halves[0:1], "blk", axis=0, tiled=True)
+    parts = [gather_blk(chunked[part]) for part in range(CHUNKS // 2, CHUNKS)] + [offloaded]
     pieces = []
-    for part in range(CHUNKS):
-        portion = gather_blk(chunked[part])
-        running = jnp.zeros((SLOTS, group_rows, chunk), jnp.float32)
+    for portion in parts:
+        width = portion.shape[2]
+        running = jnp.zeros((SLOTS, group_rows, width), jnp.float32)
         for offset in range(portion.shape[0]):
             rows_in = lax.dynamic_index_in_dim(masked, column_cd[offset], 0, keepdims=False)
             product = jnp.dot(rows_in, portion[offset], preferred_element_type=jnp.float32)
@@ -122,7 +125,7 @@
             earlier = lax.dynamic_index_in_dim(running, slot, 0, keepdims=False)
             running = lax.dynamic_update_index_in_dim(running, earlier + product, slot, 0)
         arrived = lax.all_to_all(
-            running.reshape(SLOTS, grp_count, owner_rows, chunk),
+            running.reshape(SLOTS, grp_count, owner_rows, width),
             "grp",
             split_axis=1,
             concat_axis=1,
@@ -133,6 +136,7 @@
                 "nsg,sgrc->rnc", onehot, arrived, precision=lax.Precision.HIGHEST, preferred_element_type=jnp.float32
             )
         )
+    pieces = pieces[-1:] + pieces[:-1]
     summed = jnp.concatenate(pieces, axis=2)
     return residual_in + summed
 

time: 427 us -> 388 us (0.909); the launches traced: 420 us -> 387 us
  Pallas kernels: 224 us -> 131 us
  waiting for transfers between devices: 39.1 us -> 119 us
  starting transfers between devices: 42.4 us -> 25.5 us
  matrix products: 46.3 us -> 30.4 us
  between operations: 30.9 us -> 43.9 us
    pallas_call x4 -> x2, Pallas kernels: 224 us -> 131 us  [gather_blk(): pl.pallas_call(functools.partial(gather_kernel, count), out_shape=jax.Sha...]
    all_to_all x4 -> x3, waiting for transfers between devices: 39.1 us -> 119 us  [shards(): lax.all_to_all(running.reshape(SLOTS, grp_count, owner_rows, width), 'grp...]
    all_to_all x4 -> x3, starting transfers between devices: 42.4 us -> 25.5 us  [shards(): lax.all_to_all(running.reshape(SLOTS, grp_count, owner_rows, width), 'grp...]
    dot_general x32 -> x24, matrix products: 33.4 us -> 18.2 us  [shards(): jnp.dot(rows_in, portion[offset], preferred_element_type=jnp.float32)]
    reshape x4 -> x3, local copies, waits for them, and re-layouts: 12.5 us -> 11.7 us  [shards(): running.reshape(SLOTS, grp_count, owner_rows, width)]
    dot_general x4 -> x3, matrix products: 12.8 us -> 12.2 us  [shards(): jnp.einsum('nsg,sgrc->rnc', onehot, arrived, precision=lax.Precision.HIGH...]
  transfers between devices with their start and end apart: 4 -> 4, of which waited for: 1 -> 2; matrix products, arithmetic and copies ran while one was open for 10% -> 13% of each run, Pallas kernels for 40% -> 34%
where the time goes in v7:
time: 388 us; the launch traced here: 387 us
  Pallas kernels  131 us (34%)
  waiting for transfers between devices  119 us (31%)
  between operations  43.9 us (11%)
  matrix products  30.4 us (8%)
  local copies, waits for them, and re-layouts  30.1 us (8%)
  starting transfers between devices  25.5 us (7%)
  other arithmetic  6.86 us (2%)
    pallas_call x2, Pallas kernels, gather_blk(): pl.pallas_call(functools.partial(gather_kernel, count), out_shape=jax.Sha...  131 us
    all_to_all x3, waiting for transfers between devices, shards(): lax.all_to_all(running.reshape(SLOTS, grp_count, owner_rows, width), 'grp...  119 us
    all_to_all x3, starting transfers between devices, shards(): lax.all_to_all(running.reshape(SLOTS, grp_count, owner_rows, width), 'grp...  25.5 us
    dot_general x24, matrix products, shards(): jnp.dot(rows_in, portion[offset], preferred_element_type=jnp.float32)  18.2 us
    dot_general x3, matrix products, shards(): jnp.einsum('nsg,sgrc->rnc', onehot, arrived, precision=lax.Precision.HIGH...  12.2 us
    reshape x3, local copies, waits for them, and re-layouts, shards(): running.reshape(SLOTS, grp_count, owner_rows, width)  11.7 us
  transfers between devices with their start and end apart: 4, of which 2 were waited for; matrix products, arithmetic and copies ran while one was open for 13% of the time, Pallas kernels for 34%

profile of v7, /device:TPU:1, one launch (start us, length us, event | category | flops | bytes accessed | tf_op | source)
XLA Modules:
  0.0 386.6 jit_solution(17784013174469212335)
XLA Ops:
  6.5 2.9 copy.56
  9.5 1.3 copy.57
  11.1 0.7 iota_reduce_fusion.1
  12.0 0.7 fusion.171
  14.0 0.6 fusion.170
  33.5 2.6 copy.62
  36.0 2.3 slice_bitcast_fusion.17
  38.3 73.8 %shard_map.65 = bf16[8,1024,256]{2,1,0:T(8,128)(2,1)} custom-call(bf16[1024,256]{1,0:T(8,128)(2,1)} %get-tuple-element.10.source), custom_call_target="tpu_custom_call" | custom-call | bytes 8388608 | tf_op jit(solution)/shard_map/pallas_call | solution.py:83
  122.1 2.7 broadcast_multiply_fusion
  125.0 0.6 copy-done.3
  126.0 0.4 fusion.43
  127.0 0.4 fusion.39
  127.5 0.4 fusion.37
  129.5 3.1 copy.66
  132.6 9.9 %all-to-all-start.2 = ((f32[4,32,16,256]{3,0,2,1:T(4,128)}), f32[4,32,16,256]{3,0,2,1:T(4,128)S(1)}, u32[]{:S(2)}, u32[]{:S(2)}) async-start(f32[4,32,16,256]{3,0,2,1:T(4,128)} %copy.66), calls=%async_computation.2 | async-start | bytes 4194304 | tf_op jit(solution)/shard_map/all_to_all | solution.py:127
  142.5 57.0 %shard_map.64 = bf16[8,1024,256]{2,1,0:T(8,128)(2,1)} custom-call(bf16[1024,256]{1,0:T(8,128)(2,1)} %get-tuple-element.9.source), custom_call_target="tpu_custom_call" | custom-call | bytes 8388608 | tf_op jit(solution)/shard_map/pallas_call | solution.py:83
  199.7 1.9 fusion.59
  201.7 0.5 copy-done.1
  202.2 1.7 fusion.57
  204.0 0.4 fusion.55
  204.5 0.5 fusion.53
  205.0 0.4 fusion.51
  205.5 0.4 fusion.49
  206.0 0.4 fusion.47
  206.5 0.5 fusion.45
  207.0 3.1 copy.63
  210.1 10.7 %all-to-all-start.1 = ((f32[4,32,16,256]{3,0,2,1:T(4,128)}), f32[4,32,16,256]{3,0,2,1:T(4,128)}, u32[]{:S(2)}, u32[]{:S(2)}) async-start(f32[4,32,16,256]{3,0,2,1:T(4,128)} %copy.63), calls=%async_computation.1 | async-start | bytes 4194304 | tf_op jit(solution)/shard_map/all_to_all | solution.py:127
  220.8 0.5 broadcast_in_dim.96
  221.3 1.7 copy-done.2
  223.0 1.9 fusion.23
  225.0 2.1 fusion.22
  227.2 1.4 copy-done.5
  228.6 0.7 fusion.20
  229.4 0.7 fusion.18
  230.2 0.7 fusion.16
  231.0 0.7 fusion.14
  231.8 0.7 fusion.12
  232.6 0.7 fusion.10
  233.3 5.5 %copy.58 = f32[4,32,16,512]{3,0,2,1:T(4,128)} copy(f32[4,32,16,512]{3,2,1,0:T(8,128)S(1)} %bitcast.319) | data formatting | bytes 8388608 | tf_op jit(solution)/shard_map/reshape | solution.py:128
  238.9 31.9 %all-to-all-done.1 = f32[4,32,16,256]{3,0,2,1:T(4,128)} async-done(((f32[4,32,16,256]{3,0,2,1:T(4,128)}), f32[4,32,16,256]{3,0,2,1:T(4,128)}, u32[]{:S(2)}, u32[]{:S(2)}) %all-to-all-start.1) | async-done | bytes 2097184 | tf_op jit(solution)/shard_map/all_to_all | solution.py:127
  270.8 5.0 %all-to-all-start = ((f32[4,32,16,512]{3,0,2,1:T(4,128)}), f32[4,32,16,512]{3,0,2,1:T(4,128)}, u32[]{:S(2)}, u32[]{:S(2)}) async-start(f32[4,32,16,512]{3,0,2,1:T(4,128)} %copy.58), calls=%async_computation | async-start | bytes 8388608 | tf_op jit(solution)/shard_map/all_to_all | solution.py:127
  275.8 0.6 iota_reduce_fusion
  276.8 2.1 fusion.27
  279.1 3.5 fusion.24
  282.9 86.9 %all-to-all-done = f32[4,32,16,512]{3,0,2,1:T(4,128)} async-done(((f32[4,32,16,512]{3,0,2,1:T(4,128)}), f32[4,32,16,512]{3,0,2,1:T(4,128)}, u32[]{:S(2)}, u32[]{:S(2)}) %all-to-all-start) | async-done | bytes 4194336 | tf_op jit(solution)/shard_map/all_to_all | solution.py:127
  369.8 6.6 %fusion.6 = f32[16,512,50]{1,2,0:T(8,128)S(1)} fusion(f32[4,32,16,512]{3,0,2,1:T(4,128)} %all-to-all-done, pred[50,4,32]{0,2,1:T(8,128)(4,1)S(1)} %and_reduce_fusion), kind=kOutput, calls=%fused_computation.9 | convolution fusion | flops 629145600 | bytes 5839104 | tf_op jit(solution)/shard_map/nsg,sgrc->rnc/dot_general | solution.py:135
  376.4 1.0 copy.87
  377.4 2.3 maximum_add_fusion
  (62 shorter events, 5.2 us)
Async XLA Ops:
  6.5 4.4 %copy-start.8 = (s32[8,32]{1,0:T(8,128)S(1)}, s32[8,32]{1,0:T(8,128)}, u32[]{:S(2)}) copy-start(s32[8,32]{1,0:T(8,128)} %param.10) | copy-start | bytes 3076
  6.5 4.4 %copy-start.7 = (s32[8,32]{1,0:T(8,128)S(1)}, s32[8,32]{1,0:T(8,128)}, u32[]{:S(2)}) copy-start(s32[8,32]{1,0:T(8,128)} %param.9) | copy-start | bytes 3076
  6.5 26.7 %copy-start.9 = (s32[4,32]{1,0:T(4,128)S(1)}, s32[4,32]{1,0:T(4,128)}, u32[]{:S(2)}) copy-start(s32[4,32]{1,0:T(4,128)} %param.7) | copy-start | bytes 1540
  6.5 214.2 %all-gather.2.cloned.1.call-start = ((), (), s32[]{:S(2)}) async-start(), calls=%async_computation.3 | async-start | bytes 9437184 | tf_op jit(solution)/shard_map/all_gather | solution.py:115
  122.1 3.5 copy-start.3
  124.8 4.3 %copy-start = (bf16[4,512,1024]{2,1,0:T(8,128)(2,1)}, bf16[4,512,1024]{2,1,0:T(8,128)(2,1)S(1)}, u32[]{:S(2)}) copy-start(bf16[4,512,1024]{2,1,0:T(8,128)(2,1)S(1)} %broadcast_multiply_fusion) | copy-start | bytes 12582916
  132.6 77.5 %all-to-all-start.2 = ((f32[4,32,16,256]{3,0,2,1:T(4,128)}), f32[4,32,16,256]{3,0,2,1:T(4,128)S(1)}, u32[]{:S(2)}, u32[]{:S(2)}) async-start(f32[4,32,16,256]{3,0,2,1:T(4,128)} %copy.66), calls=%async_computation.2 | async-start | bytes 4194304 | tf_op jit(solution)/shard_map/all_to_all | solution.py:127
  199.5 2.7 copy-start.1
  199.5 4.5 %copy-start.4 = (bf16[8,1024,256]{2,1,0:T(8,128)(2,1)S(1)}, bf16[8,1024,256]{2,1,0:T(8,128)(2,1)}, u32[]{:S(2)}) copy-start(bf16[8,1024,256]{2,1,0:T(8,128)(2,1)} %shard_map.64) | copy-start | bytes 12582916
  210.1 60.7 %all-to-all-start.1 = ((f32[4,32,16,256]{3,0,2,1:T(4,128)}), f32[4,32,16,256]{3,0,2,1:T(4,128)}, u32[]{:S(2)}, u32[]{:S(2)}) async-start(f32[4,32,16,256]{3,0,2,1:T(4,128)} %copy.63), calls=%async_computation.1 | async-start | bytes 4194304 | tf_op jit(solution)/shard_map/all_to_all | solution.py:127
  220.8 2.2 copy-start.2
  224.9 3.7 copy-start.5
  270.8 99.0 %all-to-all-start = ((f32[4,32,16,512]{3,0,2,1:T(4,128)}), f32[4,32,16,512]{3,0,2,1:T(4,128)}, u32[]{:S(2)}, u32[]{:S(2)}) async-start(f32[4,32,16,512]{3,0,2,1:T(4,128)} %copy.58), calls=%async_computation | async-start | bytes 8388608 | tf_op jit(solution)/shard_map/all_to_all | solution.py:127
  369.8 7.6 %copy-start.6 = (f32[16,50,1024]{2,0,1:T(8,128)S(1)}, f32[16,50,1024]{2,0,1:T(8,128)}, u32[]{:S(2)}) copy-start(f32[16,50,1024]{2,0,1:T(8,128)} %param.11) | copy-start | bytes 9830404
Sparse Core Ops, SparseCore 0:
  11.0 117.0 all-gather.1

commit v8 on v7

--- a/solution.py
+++ b/solution.py
@@ -113,9 +113,9 @@
     chunked = jnp.transpose(integrals.reshape(integrals.shape[1], CHUNKS, chunk), (1, 0, 2))
     halves = jnp.transpose(integrals.reshape(integrals.shape[1], 2, tile_width // 2), (1, 0, 2))
     offloaded = lax.all_gather(halves[0:1], "blk", axis=0, tiled=True)
-    parts = [gather_blk(chunked[part]) for part in range(CHUNKS // 2, CHUNKS)] + [offloaded]
     pieces = []
-    for portion in parts:
+
+    def contract(portion):
         width = portion.shape[2]
         running = jnp.zeros((SLOTS, group_rows, width), jnp.float32)
         for offset in range(portion.shape[0]):
@@ -124,6 +124,10 @@
             slot = column_slot[offset]
             earlier = lax.dynamic_index_in_dim(running, slot, 0, keepdims=False)
             running = lax.dynamic_update_index_in_dim(running, earlier + product, slot, 0)
+        return running
+
+    def exchange(running):
+        width = running.shape[2]
         arrived = lax.all_to_all(
             running.reshape(SLOTS, grp_count, owner_rows, width),
             "grp",
@@ -131,12 +135,14 @@
             concat_axis=1,
             tiled=True,
         )
-        pieces.append(
-            jnp.einsum(
-                "nsg,sgrc->rnc", onehot, arrived, precision=lax.Precision.HIGHEST, preferred_element_type=jnp.float32
-            )
+        return jnp.einsum(
+            "nsg,sgrc->rnc", onehot, arrived, precision=lax.Precision.HIGHEST, preferred_element_type=jnp.float32
         )
-    pieces = pieces[-1:] + pieces[:-1]
+
+    first = exchange(contract(gather_blk(chunked[CHUNKS // 2])))
+    offloaded_sums = contract(offloaded)
+    offloaded_sums, last_input = lax.optimization_barrier((offloaded_sums, chunked[CHUNKS - 1]))
+    pieces = [exchange(offloaded_sums), first, exchange(contract(gather_blk(last_input)))]
     summed = jnp.concatenate(pieces, axis=2)
     return residual_in + summed
 

time: 388 us -> 403 us (1.039)
  waiting for transfers between devices: 119 us -> 129 us
  local copies, waits for them, and re-layouts: 30.1 us -> 34.4 us
    all_to_all x3, waiting for transfers between devices: 119 us -> 129 us  [exchange(): lax.all_to_all(running.reshape(SLOTS, grp_count, owner_rows, width), 'grp...]
    unnamed x21 -> x23, local copies, waits for them, and re-layouts: 7.03 us -> 8.95 us
  transfers between devices with their start and end apart: 4 -> 4, of which waited for: 2 -> 2; matrix products, arithmetic and copies ran while one was open for 13% -> 13% of each run, Pallas kernels for 34% -> 33%
where the time goes in v8:
time: 403 us; the launch traced here: 401 us
  Pallas kernels  133 us (33%)
  waiting for transfers between devices  129 us (32%)
  between operations  43.9 us (11%)
  local copies, waits for them, and re-layouts  34.4 us (9%)
  matrix products  30.4 us (8%)
  starting transfers between devices  23.2 us (6%)
  other arithmetic  6.86 us (2%)
    pallas_call x2, Pallas kernels, gather_blk(): pl.pallas_call(functools.partial(gather_kernel, count), out_shape=jax.Sha...  133 us
    all_to_all x3, waiting for transfers between devices, exchange(): lax.all_to_all(running.reshape(SLOTS, grp_count, owner_rows, width), 'grp...  129 us
    all_to_all x3, starting transfers between devices, exchange(): lax.all_to_all(running.reshape(SLOTS, grp_count, owner_rows, width), 'grp...  23.2 us
    dot_general x24, matrix products, contract(): jnp.dot(rows_in, portion[offset], preferred_element_type=jnp.float32)  18.2 us
    reshape x3, local copies, waits for them, and re-layouts, exchange(): running.reshape(SLOTS, grp_count, owner_rows, width)  14 us
    dot_general x3, matrix products, exchange(): jnp.einsum('nsg,sgrc->rnc', onehot, arrived, precision=lax.Precision.HIGH...  12.2 us
    unnamed x23, local copies, waits for them, and re-layouts  8.95 us
  transfers between devices with their start and end apart: 4, of which 2 were waited for; matrix products, arithmetic and copies ran while one was open for 13% of the time, Pallas kernels for 33%

profile of v8, /device:TPU:1, one launch (start us, length us, event | category | flops | bytes accessed | tf_op | source)
XLA Modules:
  0.0 401.0 jit_solution(5395497324294172259)
XLA Ops:
  6.5 2.9 copy.56
  9.5 1.3 copy.57
  11.1 0.7 iota_reduce_fusion.1
  12.0 0.7 fusion.171
  14.0 0.6 fusion.170
  33.5 2.6 copy.59
  36.0 2.3 slice_bitcast_fusion.16
  38.3 73.8 %shard_map.64 = bf16[8,1024,256]{2,1,0:T(8,128)(2,1)} custom-call(bf16[1024,256]{1,0:T(8,128)(2,1)} %get-tuple-element.13.source), custom_call_target="tpu_custom_call" | custom-call | bytes 8388608 | tf_op jit(solution)/shard_map/pallas_call | solution.py:83
  122.1 2.7 broadcast_multiply_fusion
  124.9 0.6 copy-done.4
  126.0 0.4 fusion.57
  127.5 0.4 fusion.51
  129.5 3.2 copy.63
  132.7 9.9 %all-to-all-start.1 = ((f32[4,32,16,256]{3,0,2,1:T(4,128)}), f32[4,32,16,256]{3,0,2,1:T(4,128)S(1)}, u32[]{:S(2)}, u32[]{:S(2)}) async-start(f32[4,32,16,256]{3,0,2,1:T(4,128)} %copy.63), calls=%async_computation.1 | async-start | bytes 4194304 | tf_op jit(solution)/shard_map/all_to_all | solution.py:131
  142.6 0.5 broadcast_in_dim.96
  143.1 1.7 copy-done.1
  144.8 1.9 fusion.23
  146.8 2.1 fusion.22
  149.0 1.4 copy-done.6
  150.4 0.7 fusion.20
  151.2 0.7 fusion.18
  152.0 0.7 fusion.16
  152.8 0.7 fusion.14
  153.6 0.7 fusion.12
  154.4 0.7 fusion.10
  155.1 1.9 copy-done.3
  157.0 59.1 %shard_map.65 = bf16[8,1024,256]{2,1,0:T(8,128)(2,1)} custom-call(bf16[1024,256]{1,0:T(8,128)(2,1)} %get-tuple-element.12.source), custom_call_target="tpu_custom_call" | custom-call | bytes 8388608 | tf_op jit(solution)/shard_map/pallas_call | solution.py:83
  216.3 1.9 fusion.58
  218.4 0.5 copy-done.2
  218.8 1.7 fusion.43
  220.6 0.5 fusion.41
  221.1 0.4 fusion.39
  221.7 0.4 fusion.37
  222.2 0.5 fusion.35
  222.7 0.4 fusion.33
  223.2 0.4 fusion.31
  223.6 3.1 copy.66
  226.7 8.4 %all-to-all-start.2 = ((f32[4,32,16,256]{3,0,2,1:T(4,128)}), f32[4,32,16,256]{3,0,2,1:T(4,128)}, u32[]{:S(2)}, u32[]{:S(2)}) async-start(f32[4,32,16,256]{3,0,2,1:T(4,128)} %copy.66), calls=%async_computation.2 | async-start | bytes 4194304 | tf_op jit(solution)/shard_map/all_to_all | solution.py:131
  235.1 7.8 %copy.60 = f32[4,32,16,512]{3,0,2,1:T(4,128)} copy(f32[4,32,16,512]{3,2,1,0:T(8,128)} %bitcast.319) | data formatting | bytes 8388608 | tf_op jit(solution)/shard_map/reshape | solution.py:132
  242.9 42.4 %all-to-all-done.2 = f32[4,32,16,256]{3,0,2,1:T(4,128)} async-done(((f32[4,32,16,256]{3,0,2,1:T(4,128)}), f32[4,32,16,256]{3,0,2,1:T(4,128)}, u32[]{:S(2)}, u32[]{:S(2)}) %all-to-all-start.2) | async-done | bytes 2097184 | tf_op jit(solution)/shard_map/all_to_all | solution.py:131
  285.3 4.9 %all-to-all-start = ((f32[4,32,16,512]{3,0,2,1:T(4,128)}), f32[4,32,16,512]{3,0,2,1:T(4,128)}, u32[]{:S(2)}, u32[]{:S(2)}) async-start(f32[4,32,16,512]{3,0,2,1:T(4,128)} %copy.60), calls=%async_computation | async-start | bytes 8388608 | tf_op jit(solution)/shard_map/all_to_all | solution.py:131
  290.2 0.6 iota_reduce_fusion
  291.2 2.1 fusion.24
  293.5 3.5 fusion.27
  297.3 86.8 %all-to-all-done = f32[4,32,16,512]{3,0,2,1:T(4,128)} async-done(((f32[4,32,16,512]{3,0,2,1:T(4,128)}), f32[4,32,16,512]{3,0,2,1:T(4,128)}, u32[]{:S(2)}, u32[]{:S(2)}) %all-to-all-start) | async-done | bytes 4194336 | tf_op jit(solution)/shard_map/all_to_all | solution.py:131
  384.2 6.6 %fusion.6 = f32[16,512,50]{1,2,0:T(8,128)S(1)} fusion(f32[4,32,16,512]{3,0,2,1:T(4,128)} %all-to-all-done, pred[50,4,32]{0,2,1:T(8,128)(4,1)S(1)} %and_reduce_fusion), kind=kOutput, calls=%fused_computation.9 | convolution fusion | flops 629145600 | bytes 5839104 | tf_op jit(solution)/shard_map/nsg,sgrc->rnc/dot_general | solution.py:138
  390.8 1.0 copy.87
  391.8 2.3 maximum_add_fusion
  (64 shorter events, 5.7 us)
Async XLA Ops:
  6.5 4.4 %copy-start.9 = (s32[8,32]{1,0:T(8,128)S(1)}, s32[8,32]{1,0:T(8,128)}, u32[]{:S(2)}) copy-start(s32[8,32]{1,0:T(8,128)} %param.10) | copy-start | bytes 3076
  6.5 4.4 %copy-start.8 = (s32[8,32]{1,0:T(8,128)S(1)}, s32[8,32]{1,0:T(8,128)}, u32[]{:S(2)}) copy-start(s32[8,32]{1,0:T(8,128)} %param.9) | copy-start | bytes 3076
  6.5 26.7 %copy-start.10 = (s32[4,32]{1,0:T(4,128)S(1)}, s32[4,32]{1,0:T(4,128)}, u32[]{:S(2)}) copy-start(s32[4,32]{1,0:T(4,128)} %param.7) | copy-start | bytes 1540
  6.5 136.0 %all-gather.2.cloned.1.call-start = ((), (), s32[]{:S(2)}) async-start(), calls=%async_computation.3 | async-start | bytes 9437184 | tf_op jit(solution)/shard_map/all_gather | solution.py:115
  122.1 3.5 copy-start.4
  124.8 4.3 %copy-start = (bf16[4,512,1024]{2,1,0:T(8,128)(2,1)}, bf16[4,512,1024]{2,1,0:T(8,128)(2,1)S(1)}, u32[]{:S(2)}) copy-start(bf16[4,512,1024]{2,1,0:T(8,128)(2,1)S(1)} %broadcast_multiply_fusion) | copy-start | bytes 12582916
  132.7 94.1 %all-to-all-start.1 = ((f32[4,32,16,256]{3,0,2,1:T(4,128)}), f32[4,32,16,256]{3,0,2,1:T(4,128)S(1)}, u32[]{:S(2)}, u32[]{:S(2)}) async-start(f32[4,32,16,256]{3,0,2,1:T(4,128)} %copy.63), calls=%async_computation.1 | async-start | bytes 4194304 | tf_op jit(solution)/shard_map/all_to_all | solution.py:131
  142.6 2.2 copy-start.1
  146.7 3.7 copy-start.6
  155.1 1.9 copy-start.3
  216.2 2.7 copy-start.2
  216.2 4.5 %copy-start.5 = (bf16[8,1024,256]{2,1,0:T(8,128)(2,1)S(1)}, bf16[8,1024,256]{2,1,0:T(8,128)(2,1)}, u32[]{:S(2)}) copy-start(bf16[8,1024,256]{2,1,0:T(8,128)(2,1)} %shard_map.65) | copy-start | bytes 12582916
  226.7 58.5 %all-to-all-start.2 = ((f32[4,32,16,256]{3,0,2,1:T(4,128)}), f32[4,32,16,256]{3,0,2,1:T(4,128)}, u32[]{:S(2)}, u32[]{:S(2)}) async-start(f32[4,32,16,256]{3,0,2,1:T(4,128)} %copy.66), calls=%async_computation.2 | async-start | bytes 4194304 | tf_op jit(solution)/shard_map/all_to_all | solution.py:131
  285.3 98.9 %all-to-all-start = ((f32[4,32,16,512]{3,0,2,1:T(4,128)}), f32[4,32,16,512]{3,0,2,1:T(4,128)}, u32[]{:S(2)}, u32[]{:S(2)}) async-start(f32[4,32,16,512]{3,0,2,1:T(4,128)} %copy.60), calls=%async_computation | async-start | bytes 8388608 | tf_op jit(solution)/shard_map/all_to_all | solution.py:131
  384.2 7.6 %copy-start.7 = (f32[16,50,1024]{2,0,1:T(8,128)S(1)}, f32[16,50,1024]{2,0,1:T(8,128)}, u32[]{:S(2)}) copy-start(f32[16,50,1024]{2,0,1:T(8,128)} %param.11) | copy-start | bytes 9830404
Sparse Core Ops, SparseCore 0:
  11.0 116.9 all-gather.1

commit v9 on v7

--- a/solution.py
+++ b/solution.py
@@ -111,9 +111,8 @@
     onehot = jnp.any(ab_hit[:, :, None, :] & slot_hit[None, :, :, :], axis=1).astype(jnp.float32)
     chunk = tile_width // CHUNKS
     chunked = jnp.transpose(integrals.reshape(integrals.shape[1], CHUNKS, chunk), (1, 0, 2))
-    halves = jnp.transpose(integrals.reshape(integrals.shape[1], 2, tile_width // 2), (1, 0, 2))
-    offloaded = lax.all_gather(halves[0:1], "blk", axis=0, tiled=True)
-    parts = [gather_blk(chunked[part]) for part in range(CHUNKS // 2, CHUNKS)] + [offloaded]
+    offloaded = lax.all_gather(chunked[0:1], "blk", axis=0, tiled=True)
+    parts = [gather_blk(chunked[part]) for part in range(1, CHUNKS)] + [offloaded]
     pieces = []
     for portion in parts:
         width = portion.shape[2]

time: 388 us -> 431 us (1.11); the launches traced: 387 us -> 424 us
  Pallas kernels: 131 us -> 190 us
  waiting for transfers between devices: 119 us -> 79 us
  starting transfers between devices: 25.5 us -> 34.7 us
  matrix products: 30.4 us -> 38.2 us
    pallas_call x2 -> x3, Pallas kernels: 131 us -> 190 us  [gather_blk(): pl.pallas_call(functools.partial(gather_kernel, count), out_shape=jax.Sha...]
    all_to_all x3 -> x4, waiting for transfers between devices: 119 us -> 78.3 us  [shards(): lax.all_to_all(running.reshape(SLOTS, grp_count, owner_rows, width), 'grp...]
    all_to_all x3 -> x4, starting transfers between devices: 25.5 us -> 34.7 us  [shards(): lax.all_to_all(running.reshape(SLOTS, grp_count, owner_rows, width), 'grp...]
    dot_general x24 -> x32, matrix products: 18.2 us -> 25.4 us  [shards(): jnp.dot(rows_in, portion[offset], preferred_element_type=jnp.float32)]
    reshape x3 -> x4, local copies, waits for them, and re-layouts: 11.7 us -> 12.5 us  [shards(): running.reshape(SLOTS, grp_count, owner_rows, width)]
    dot_general x3 -> x4, matrix products: 12.2 us -> 12.8 us  [shards(): jnp.einsum('nsg,sgrc->rnc', onehot, arrived, precision=lax.Precision.HIGH...]
  transfers between devices with their start and end apart: 4 -> 5, of which waited for: 2 -> 2; matrix products, arithmetic and copies ran while one was open for 13% -> 10% of each run, Pallas kernels for 34% -> 32%
where the time goes in v9:
time: 431 us; the launch traced here: 424 us
  Pallas kernels  190 us (44%)
  waiting for transfers between devices  79 us (18%)
  between operations  44.4 us (10%)
  matrix products  38.2 us (9%)
  starting transfers between devices  34.7 us (8%)
  local copies, waits for them, and re-layouts  28.5 us (7%)
  other arithmetic  9.47 us (2%)
    pallas_call x3, Pallas kernels, gather_blk(): pl.pallas_call(functools.partial(gather_kernel, count), out_shape=jax.Sha...  190 us
    all_to_all x4, waiting for transfers between devices, shards(): lax.all_to_all(running.reshape(SLOTS, grp_count, owner_rows, width), 'grp...  78.3 us
    all_to_all x4, starting transfers between devices, shards(): lax.all_to_all(running.reshape(SLOTS, grp_count, owner_rows, width), 'grp...  34.7 us
    dot_general x32, matrix products, shards(): jnp.dot(rows_in, portion[offset], preferred_element_type=jnp.float32)  25.4 us
    dot_general x4, matrix products, shards(): jnp.einsum('nsg,sgrc->rnc', onehot, arrived, precision=lax.Precision.HIGH...  12.8 us
    reshape x4, local copies, waits for them, and re-layouts, shards(): running.reshape(SLOTS, grp_count, owner_rows, width)  12.5 us
  transfers between devices with their start and end apart: 5, of which 2 were waited for; matrix products, arithmetic and copies ran while one was open for 10% of the time, Pallas kernels for 32%

profile of v9, /device:TPU:1, one launch (start us, length us, event | category | flops | bytes accessed | tf_op | source)
XLA Modules:
  0.0 424.3 jit_solution(16190048248256432165)
XLA Ops:
  6.5 0.9 constant_dynamic-slice_fusion.29
  7.4 0.7 iota_reduce_fusion.1
  8.3 0.7 fusion.233
  10.1 0.6 fusion.232
  29.6 0.7 convert_element_type.18
  30.5 3.9 copy.41
  34.4 2.8 copy.42
  37.2 1.3 fusion.231
  38.6 54.7 %shard_map.64 = bf16[8,1024,256]{2,1,0:T(8,128)(2,1)} custom-call(bf16[1024,256]{1,0:T(8,128)(2,1)} %get-tuple-element.12.source), custom_call_target="tpu_custom_call" | custom-call | bytes 8388608 | tf_op jit(solution)/shard_map/pallas_call | solution.py:83
  94.5 4.5 %broadcast_multiply_fusion = bf16[4,512,1024]{2,1,0:T(8,128)(2,1)} fusion(bf16[4,512,1024]{2,1,0:T(8,128)(2,1)} %param.6, bf16[4,512]{1,0:T(4,128)(2,1)S(1)} %convert_element_type.19), kind=kLoop, calls=%fused_computation.9 | loop fusion | flops 2097152 | bytes 8392704 | tf_op jit(solution)/shard_map/mul | solution.py:104
  107.9 1.9 fusion.78
  109.9 0.5 copy-done
  110.4 1.7 fusion.61
  113.8 0.5 fusion.53
  115.3 3.1 copy.46
  118.4 9.4 %all-to-all-start.1 = ((f32[4,32,16,256]{3,0,2,1:T(4,128)}), f32[4,32,16,256]{3,0,2,1:T(4,128)S(1)}, u32[]{:S(2)}, u32[]{:S(2)}) async-start(f32[4,32,16,256]{3,0,2,1:T(4,128)} %copy.46), calls=%async_computation.1 | async-start | bytes 4194304 | tf_op jit(solution)/shard_map/all_to_all | solution.py:126
  127.8 0.7 all-gather.2.cloned.1.call-update
  128.5 78.6 %shard_map.65 = bf16[8,1024,256]{2,1,0:T(8,128)(2,1)} custom-call(bf16[1024,256]{1,0:T(8,128)(2,1)} %get-tuple-element.11.source), custom_call_target="tpu_custom_call" | custom-call | bytes 8388608 | tf_op jit(solution)/shard_map/pallas_call | solution.py:83
  207.3 2.0 fusion.77
  209.3 0.5 copy-done.1
  209.8 1.7 fusion.47
  213.3 0.5 fusion.39
  214.7 3.1 copy.49
  217.9 8.3 %all-to-all-start.2 = ((f32[4,32,16,256]{3,0,2,1:T(4,128)}), f32[4,32,16,256]{3,0,2,1:T(4,128)}, u32[]{:S(2)}, u32[]{:S(2)}) async-start(f32[4,32,16,256]{3,0,2,1:T(4,128)} %copy.49), calls=%async_computation.2 | async-start | bytes 4194304 | tf_op jit(solution)/shard_map/all_to_all | solution.py:126
  226.2 56.6 %shard_map.66 = bf16[8,1024,256]{2,1,0:T(8,128)(2,1)} custom-call(bf16[1024,256]{1,0:T(8,128)(2,1)} %get-tuple-element.10.source), custom_call_target="tpu_custom_call" | custom-call | bytes 8388608 | tf_op jit(solution)/shard_map/pallas_call | solution.py:83
  283.0 1.9 fusion.76
  285.0 0.5 copy-done.2
  285.5 1.7 fusion.33
  287.9 0.5 fusion.29
  289.4 0.5 fusion.23
  290.4 3.1 copy.52
  293.5 12.1 %all-to-all-start.3 = ((f32[4,32,16,256]{3,0,2,1:T(4,128)}), f32[4,32,16,256]{3,0,2,1:T(4,128)}, u32[]{:S(2)}, u32[]{:S(2)}) async-start(f32[4,32,16,256]{3,0,2,1:T(4,128)} %copy.52), calls=%async_computation.3 | async-start | bytes 4194304 | tf_op jit(solution)/shard_map/all_to_all | solution.py:126
  305.8 2.0 fusion.79
  307.9 0.5 copy-done.3
  308.3 1.7 fusion.75
  311.8 0.5 fusion.67
  312.3 0.5 fusion.65
  312.8 0.5 fusion.63
  313.3 3.1 copy.43
  316.4 39.1 %all-to-all-done.3 = f32[4,32,16,256]{3,0,2,1:T(4,128)} async-done(((f32[4,32,16,256]{3,0,2,1:T(4,128)}), f32[4,32,16,256]{3,0,2,1:T(4,128)}, u32[]{:S(2)}, u32[]{:S(2)}) %all-to-all-start.3) | async-done | bytes 2097184 | tf_op jit(solution)/shard_map/all_to_all | solution.py:126
  355.6 4.9 %all-to-all-start = ((f32[4,32,16,256]{3,0,2,1:T(4,128)}), f32[4,32,16,256]{3,0,2,1:T(4,128)}, u32[]{:S(2)}, u32[]{:S(2)}) async-start(f32[4,32,16,256]{3,0,2,1:T(4,128)} %copy.43), calls=%async_computation | async-start | bytes 4194304 | tf_op jit(solution)/shard_map/all_to_all | solution.py:126
  360.5 0.6 iota_reduce_fusion
  361.4 2.1 fusion.11
  363.8 3.5 fusion.14
  367.6 3.5 fusion.17
  371.4 39.1 %all-to-all-done = f32[4,32,16,256]{3,0,2,1:T(4,128)} async-done(((f32[4,32,16,256]{3,0,2,1:T(4,128)}), f32[4,32,16,256]{3,0,2,1:T(4,128)}, u32[]{:S(2)}, u32[]{:S(2)}) %all-to-all-start) | async-done | bytes 2097184 | tf_op jit(solution)/shard_map/all_to_all | solution.py:126
  410.6 3.7 fusion.8
  414.5 2.5 maximum_add_fusion
  (82 shorter events, 12.1 us)
Async XLA Ops:
  107.7 2.7 copy-start
  109.8 2.5 copy-start.4
  118.4 99.4 %all-to-all-start.1 = ((f32[4,32,16,256]{3,0,2,1:T(4,128)}), f32[4,32,16,256]{3,0,2,1:T(4,128)S(1)}, u32[]{:S(2)}, u32[]{:S(2)}) async-start(f32[4,32,16,256]{3,0,2,1:T(4,128)} %copy.46), calls=%async_computation.1 | async-start | bytes 4194304 | tf_op jit(solution)/shard_map/all_to_all | solution.py:126
  127.8 177.9 %all-gather.2.cloned.1.call-start = ((), (), s32[]{:S(2)}) async-start(), calls=%async_computation.4 | async-start | bytes 4718592 | tf_op jit(solution)/shard_map/all_gather | solution.py:114
  207.1 2.7 copy-start.1
  209.3 2.5 copy-start.5
  217.9 75.7 %all-to-all-start.2 = ((f32[4,32,16,256]{3,0,2,1:T(4,128)}), f32[4,32,16,256]{3,0,2,1:T(4,128)}, u32[]{:S(2)}, u32[]{:S(2)}) async-start(f32[4,32,16,256]{3,0,2,1:T(4,128)} %copy.49), calls=%async_computation.2 | async-start | bytes 4194304 | tf_op jit(solution)/shard_map/all_to_all | solution.py:126
  282.8 2.7 copy-start.2
  284.9 2.5 copy-start.6
  293.5 62.0 %all-to-all-start.3 = ((f32[4,32,16,256]{3,0,2,1:T(4,128)}), f32[4,32,16,256]{3,0,2,1:T(4,128)}, u32[]{:S(2)}, u32[]{:S(2)}) async-start(f32[4,32,16,256]{3,0,2,1:T(4,128)} %copy.52), calls=%async_computation.3 | async-start | bytes 4194304 | tf_op jit(solution)/shard_map/all_to_all | solution.py:126
  305.7 2.7 copy-start.3
  307.8 2.5 copy-start.8
  316.4 44.1 %copy-start.9 = (s32[8,32]{1,0:T(8,128)S(1)}, s32[8,32]{1,0:T(8,128)}, u32[]{:S(2)}) copy-start(s32[8,32]{1,0:T(8,128)} %param.9) | copy-start | bytes 3076
  355.6 55.0 %all-to-all-start = ((f32[4,32,16,256]{3,0,2,1:T(4,128)}), f32[4,32,16,256]{3,0,2,1:T(4,128)}, u32[]{:S(2)}, u32[]{:S(2)}) async-start(f32[4,32,16,256]{3,0,2,1:T(4,128)} %copy.43), calls=%async_computation | async-start | bytes 4194304 | tf_op jit(solution)/shard_map/all_to_all | solution.py:126
  410.6 4.0 copy-start.7
Sparse Core Ops, SparseCore 0:
  131.3 90.3 all-gather.1

commit v10 on v7

--- a/solution.py
+++ b/solution.py
@@ -113,7 +113,7 @@
     chunked = jnp.transpose(integrals.reshape(integrals.shape[1], CHUNKS, chunk), (1, 0, 2))
     halves = jnp.transpose(integrals.reshape(integrals.shape[1], 2, tile_width // 2), (1, 0, 2))
     offloaded = lax.all_gather(halves[0:1], "blk", axis=0, tiled=True)
-    parts = [gather_blk(chunked[part]) for part in range(CHUNKS // 2, CHUNKS)] + [offloaded]
+    parts = [gather_blk(halves[1]), offloaded]
     pieces = []
     for portion in parts:
         width = portion.shape[2]

time: 388 us -> 409 us (1.054)
  waiting for transfers between devices: 119 us -> 162 us
  starting transfers between devices: 25.5 us -> 15.2 us
  Pallas kernels: 131 us -> 122 us
    all_to_all x3 -> x2, waiting for transfers between devices: 119 us -> 162 us  [shards(): lax.all_to_all(running.reshape(SLOTS, grp_count, owner_rows, width), 'grp...]
    all_to_all x3 -> x2, starting transfers between devices: 25.5 us -> 15.1 us  [shards(): lax.all_to_all(running.reshape(SLOTS, grp_count, owner_rows, width), 'grp...]
    pallas_call x2 -> x1, Pallas kernels: 131 us -> 122 us  [gather_blk(): pl.pallas_call(functools.partial(gather_kernel, count), out_shape=jax.Sha...]
    dot_general x24 -> x16, matrix products: 18.2 us -> 14 us  [shards(): jnp.dot(rows_in, portion[offset], preferred_element_type=jnp.float32)]
    unnamed x21 -> x17, local copies, waits for them, and re-layouts: 7.03 us -> 9.94 us
    dot_general x3 -> x2, matrix products: 12.2 us -> 13.1 us  [shards(): jnp.einsum('nsg,sgrc->rnc', onehot, arrived, precision=lax.Precision.HIGH...]
    reshape x3 -> x2, local copies, waits for them, and re-layouts: 11.7 us -> 11.1 us  [shards(): running.reshape(SLOTS, grp_count, owner_rows, width)]
  transfers between devices with their start and end apart: 4 -> 3, of which waited for: 2 -> 2; matrix products, arithmetic and copies ran while one was open for 13% -> 10% of each run, Pallas kernels for 34% -> 30%
where the time goes in v10:
time: 409 us; the launch traced here: 408 us
  waiting for transfers between devices  162 us (40%)
  Pallas kernels  122 us (30%)
  between operations  44 us (11%)
  local copies, waits for them, and re-layouts  31.1 us (8%)
  matrix products  27.1 us (7%)
  starting transfers between devices  15.2 us (4%)
  other arithmetic  6.89 us (2%)
    all_to_all x2, waiting for transfers between devices, shards(): lax.all_to_all(running.reshape(SLOTS, grp_count, owner_rows, width), 'grp...  162 us
    pallas_call x1, Pallas kernels, gather_blk(): pl.pallas_call(functools.partial(gather_kernel, count), out_shape=jax.Sha...  122 us
    all_to_all x2, starting transfers between devices, shards(): lax.all_to_all(running.reshape(SLOTS, grp_count, owner_rows, width), 'grp...  15.1 us
    dot_general x16, matrix products, shards(): jnp.dot(rows_in, portion[offset], preferred_element_type=jnp.float32)  14 us
    dot_general x2, matrix products, shards(): jnp.einsum('nsg,sgrc->rnc', onehot, arrived, precision=lax.Precision.HIGH...  13.1 us
    reshape x2, local copies, waits for them, and re-layouts, shards(): running.reshape(SLOTS, grp_count, owner_rows, width)  11.1 us
    unnamed x17, local copies, waits for them, and re-layouts  9.94 us
  transfers between devices with their start and end apart: 3, of which 2 were waited for; matrix products, arithmetic and copies ran while one was open for 10% of the time, Pallas kernels for 30%

profile of v10, /device:TPU:1, one launch (start us, length us, event | category | flops | bytes accessed | tf_op | source)
XLA Modules:
  0.0 407.9 jit_solution(16785764241798753531)
XLA Ops:
  6.5 3.9 copy.31
  10.5 2.9 copy.32
  13.4 1.5 fusion.109
  14.9 0.2 constant_dynamic-slice_fusion.15
  15.1 0.7 iota_reduce_fusion.1
  15.8 0.2 convert_reduce_fusion.1
  15.9 0.7 fusion.111
  17.9 0.6 fusion.110
  37.4 0.1 broadcast_in_dim.68
  37.5 0.1 convert_element_type.19
  37.6 122.1 %shard_map.64 = bf16[8,1024,512]{2,1,0:T(8,128)(2,1)} custom-call(bf16[1024,512]{1,0:T(8,128)(2,1)} %get-tuple-element.10.source), custom_call_target="tpu_custom_call" | custom-call | bytes 16777216 | tf_op jit(solution)/shard_map/pallas_call | solution.py:83
  169.7 2.7 broadcast_multiply_fusion
  172.4 0.5 broadcast.24.clone
  172.9 2.9 copy-done.2
  175.9 0.7 fusion.24
  176.6 0.1 constant_dynamic-slice_fusion.3
  176.7 0.7 fusion.23
  177.5 0.7 fusion.21
  178.3 0.7 fusion.19
  179.1 0.7 fusion.17
  179.9 0.7 fusion.15
  180.7 0.7 fusion.13
  181.5 0.7 fusion.11
  182.2 5.6 %copy.36 = f32[4,32,16,512]{3,0,2,1:T(4,128)} copy(f32[4,32,16,512]{3,2,1,0:T(8,128)S(1)} %bitcast.220) | data formatting | bytes 8388608 | tf_op jit(solution)/shard_map/reshape | solution.py:128
  187.7 7.8 %all-to-all-start.1 = ((f32[4,32,16,512]{3,0,2,1:T(4,128)}), f32[4,32,16,512]{3,0,2,1:T(4,128)}, u32[]{:S(2)}, u32[]{:S(2)}) async-start(f32[4,32,16,512]{3,0,2,1:T(4,128)} %copy.36), calls=%async_computation.1 | async-start | bytes 8388608 | tf_op jit(solution)/shard_map/all_to_all | solution.py:127
  195.6 0.5 broadcast.24.clone.1
  196.1 1.7 copy-done.1
  197.7 1.9 fusion.39
  199.8 2.1 fusion.38
  202.0 1.4 copy-done.3
  203.4 0.7 fusion.36
  204.2 0.7 fusion.34
  205.0 0.7 fusion.32
  205.8 0.7 fusion.30
  206.6 0.7 fusion.28
  207.4 0.7 fusion.26
  208.1 5.5 %copy.33 = f32[4,32,16,512]{3,0,2,1:T(4,128)} copy(f32[4,32,16,512]{3,2,1,0:T(8,128)S(1)} %bitcast.219) | data formatting | bytes 8388608 | tf_op jit(solution)/shard_map/reshape | solution.py:128
  213.6 76.0 %all-to-all-done.1 = f32[4,32,16,512]{3,0,2,1:T(4,128)} async-done(((f32[4,32,16,512]{3,0,2,1:T(4,128)}), f32[4,32,16,512]{3,0,2,1:T(4,128)}, u32[]{:S(2)}, u32[]{:S(2)}) %all-to-all-start.1) | async-done | bytes 4194336 | tf_op jit(solution)/shard_map/all_to_all | solution.py:127
  289.6 7.4 %all-to-all-start = ((f32[4,32,16,512]{3,0,2,1:T(4,128)}), f32[4,32,16,512]{3,0,2,1:T(4,128)}, u32[]{:S(2)}, u32[]{:S(2)}) async-start(f32[4,32,16,512]{3,0,2,1:T(4,128)} %copy.33), calls=%async_computation | async-start | bytes 8388608 | tf_op jit(solution)/shard_map/all_to_all | solution.py:127
  297.0 0.6 iota_reduce_fusion
  297.6 0.1 iota_compare_fusion
  297.7 0.2 and_reduce_fusion
  297.9 6.5 %fusion.7 = f32[16,512,50]{1,2,0:T(8,128)S(1)} fusion(f32[4,32,16,512]{3,0,2,1:T(4,128)} %all-to-all-done.1, pred[50,4,32]{0,2,1:T(8,128)(4,1)S(1)} %and_reduce_fusion), kind=kOutput, calls=%fused_computation.9 | convolution fusion | flops 629145600 | bytes 5839104 | tf_op jit(solution)/shard_map/nsg,sgrc->rnc/dot_general | solution.py:135
  304.4 1.0 copy.51
  305.4 85.6 %all-to-all-done = f32[4,32,16,512]{3,0,2,1:T(4,128)} async-done(((f32[4,32,16,512]{3,0,2,1:T(4,128)}), f32[4,32,16,512]{3,0,2,1:T(4,128)}, u32[]{:S(2)}, u32[]{:S(2)}) %all-to-all-start) | async-done | bytes 4194336 | tf_op jit(solution)/shard_map/all_to_all | solution.py:127
  391.0 6.6 %fusion.4 = f32[16,512,50]{1,2,0:T(8,128)S(1)} fusion(f32[4,32,16,512]{3,0,2,1:T(4,128)} %all-to-all-done, pred[50,4,32]{0,2,1:T(8,128)(4,1)S(1)} %and_reduce_fusion), kind=kOutput, calls=%fused_computation.8 | convolution fusion | flops 629145600 | bytes 5839104 | tf_op jit(solution)/shard_map/nsg,sgrc->rnc/dot_general | solution.py:135
  397.6 1.0 copy.52
  398.6 2.4 maximum_add_fusion
  (34 shorter events, 1.1 us)
Async XLA Ops:
  6.5 189.0 %all-gather.2.cloned.1.call-start = ((), (), s32[]{:S(2)}) async-start(), calls=%async_computation.2 | async-start | bytes 9437184 | tf_op jit(solution)/shard_map/all_gather | solution.py:115
  10.5 4.4 %copy-start.5 = (s32[8,32]{1,0:T(8,128)S(1)}, s32[8,32]{1,0:T(8,128)}, u32[]{:S(2)}) copy-start(s32[8,32]{1,0:T(8,128)} %param.9) | copy-start | bytes 3076
  10.5 4.4 %copy-start.6 = (s32[8,32]{1,0:T(8,128)S(1)}, s32[8,32]{1,0:T(8,128)}, u32[]{:S(2)}) copy-start(s32[8,32]{1,0:T(8,128)} %param.10) | copy-start | bytes 3076
  10.5 26.9 %copy-start.7 = (s32[4,32]{1,0:T(4,128)S(1)}, s32[4,32]{1,0:T(4,128)}, u32[]{:S(2)}) copy-start(s32[4,32]{1,0:T(4,128)} %param.7) | copy-start | bytes 1540
  169.7 6.2 %copy-start.2 = (bf16[8,1024,512]{2,1,0:T(8,128)(2,1)S(1)}, bf16[8,1024,512]{2,1,0:T(8,128)(2,1)}, u32[]{:S(2)}) copy-start(bf16[8,1024,512]{2,1,0:T(8,128)(2,1)} %shard_map.64) | copy-start | bytes 25165828
  172.4 9.1 %copy-start = (bf16[4,512,1024]{2,1,0:T(8,128)(2,1)}, bf16[4,512,1024]{2,1,0:T(8,128)(2,1)S(1)}, u32[]{:S(2)}) copy-start(bf16[4,512,1024]{2,1,0:T(8,128)(2,1)S(1)} %broadcast_multiply_fusion) | copy-start | bytes 12582916
  187.7 101.8 %all-to-all-start.1 = ((f32[4,32,16,512]{3,0,2,1:T(4,128)}), f32[4,32,16,512]{3,0,2,1:T(4,128)}, u32[]{:S(2)}, u32[]{:S(2)}) async-start(f32[4,32,16,512]{3,0,2,1:T(4,128)} %copy.36), calls=%async_computation.1 | async-start | bytes 8388608 | tf_op jit(solution)/shard_map/all_to_all | solution.py:127
  195.6 2.2 copy-start.1
  199.7 3.7 copy-start.3
  289.6 101.4 %all-to-all-start = ((f32[4,32,16,512]{3,0,2,1:T(4,128)}), f32[4,32,16,512]{3,0,2,1:T(4,128)}, u32[]{:S(2)}, u32[]{:S(2)}) async-start(f32[4,32,16,512]{3,0,2,1:T(4,128)} %copy.33), calls=%async_computation | async-start | bytes 8388608 | tf_op jit(solution)/shard_map/all_to_all | solution.py:127
  391.0 7.6 %copy-start.4 = (f32[16,50,1024]{2,0,1:T(8,128)S(1)}, f32[16,50,1024]{2,0,1:T(8,128)}, u32[]{:S(2)}) copy-start(f32[16,50,1024]{2,0,1:T(8,128)} %param.11) | copy-start | bytes 9830404
Sparse Core Ops, SparseCore 0:
  15.0 135.3 all-gather.1

commit v11 on v8

--- a/solution.py
+++ b/solution.py
@@ -113,8 +113,6 @@
     chunked = jnp.transpose(integrals.reshape(integrals.shape[1], CHUNKS, chunk), (1, 0, 2))
     halves = jnp.transpose(integrals.reshape(integrals.shape[1], 2, tile_width // 2), (1, 0, 2))
     offloaded = lax.all_gather(halves[0:1], "blk", axis=0, tiled=True)
-    pieces = []
-
     def contract(portion):
         width = portion.shape[2]
         running = jnp.zeros((SLOTS, group_rows, width), jnp.float32)
@@ -128,21 +126,24 @@
 
     def exchange(running):
         width = running.shape[2]
-        arrived = lax.all_to_all(
+        return lax.all_to_all(
             running.reshape(SLOTS, grp_count, owner_rows, width),
             "grp",
             split_axis=1,
             concat_axis=1,
             tiled=True,
         )
+
+    def accumulate(arrived):
         return jnp.einsum(
             "nsg,sgrc->rnc", onehot, arrived, precision=lax.Precision.HIGHEST, preferred_element_type=jnp.float32
         )
 
-    first = exchange(contract(gather_blk(chunked[CHUNKS // 2])))
-    offloaded_sums = contract(offloaded)
-    offloaded_sums, last_input = lax.optimization_barrier((offloaded_sums, chunked[CHUNKS - 1]))
-    pieces = [exchange(offloaded_sums), first, exchange(contract(gather_blk(last_input)))]
+    early = exchange(contract(gather_blk(chunked[CHUNKS // 2])))
+    late_sums = contract(gather_blk(chunked[CHUNKS - 1]))
+    offloaded_arrived = exchange(contract(offloaded))
+    late_sums, offloaded_arrived = lax.optimization_barrier((late_sums, offloaded_arrived))
+    pieces = [accumulate(offloaded_arrived), accumulate(early), accumulate(exchange(late_sums))]
     summed = jnp.concatenate(pieces, axis=2)
     return residual_in + summed
 

time: 403 us -> 393 us (0.975)
  Pallas kernels: 133 us -> 118 us
  local copies, waits for them, and re-layouts: 34.4 us -> 26.9 us
  waiting for transfers between devices: 129 us -> 135 us
    all_gather x1, waiting for transfers between devices: 0.02 us -> 78.7 us  [shards(): offloaded = lax.all_gather(halves[0:1], 'blk', axis=0, tiled=True)]
    all_to_all x3, waiting for transfers between devices: 129 us -> 56.7 us  [exchange(): lax.all_to_all(running.reshape(SLOTS, grp_count, owner_rows, width), 'grp...]
    pallas_call x2, Pallas kernels: 133 us -> 118 us  [gather_blk(): pl.pallas_call(functools.partial(gather_kernel, count), out_shape=jax.Sha...]
    reshape x3, local copies, waits for them, and re-layouts: 14 us -> 8.67 us  [exchange(): running.reshape(SLOTS, grp_count, owner_rows, width)]
    unnamed x23 -> x21, local copies, waits for them, and re-layouts: 8.95 us -> 6.93 us
  transfers between devices with their start and end apart: 4 -> 4, of which waited for: 2 -> 3; matrix products, arithmetic and copies ran while one was open for 13% -> 11% of each run, Pallas kernels for 33% -> 30%
where the time goes in v11:
time: 393 us; the launch traced here: 392 us
  waiting for transfers between devices  135 us (34%)
  Pallas kernels  118 us (30%)
  between operations  43.7 us (11%)
  matrix products  33 us (8%)
  local copies, waits for them, and re-layouts  26.9 us (7%)
  starting transfers between devices  25.9 us (7%)
  other arithmetic  8.74 us (2%)
    pallas_call x2, Pallas kernels, gather_blk(): pl.pallas_call(functools.partial(gather_kernel, count), out_shape=jax.Sha...  118 us
    all_gather x1, waiting for transfers between devices, shards(): offloaded = lax.all_gather(halves[0:1], 'blk', axis=0, tiled=True)  78.7 us
    all_to_all x3, waiting for transfers between devices, exchange(): lax.all_to_all(running.reshape(SLOTS, grp_count, owner_rows, width), 'grp...  56.7 us
    all_to_all x3, starting transfers between devices, exchange(): lax.all_to_all(running.reshape(SLOTS, grp_count, owner_rows, width), 'grp...  25.9 us
    dot_general x24, matrix products, contract(): jnp.dot(rows_in, portion[offset], preferred_element_type=jnp.float32)  21.1 us
    dot_general x3, matrix products, accumulate(): jnp.einsum('nsg,sgrc->rnc', onehot, arrived, precision=lax.Precision.HIGH...  11.9 us
    reshape x3, local copies, waits for them, and re-layouts, exchange(): running.reshape(SLOTS, grp_count, owner_rows, width)  8.67 us
  transfers between devices with their start and end apart: 4, of which 3 were waited for; matrix products, arithmetic and copies ran while one was open for 11% of the time, Pallas kernels for 30%

profile of v11, /device:TPU:1, one launch (start us, length us, event | category | flops | bytes accessed | tf_op | source)
XLA Modules:
  0.0 391.7 jit_solution(2875527393768670478)
XLA Ops:
  6.5 2.9 copy.56
  9.5 1.3 copy.59
  11.1 0.7 iota_reduce_fusion.1
  11.9 0.7 fusion.171
  13.9 0.6 fusion.170
  43.2 4.6 %broadcast_multiply_fusion = bf16[4,512,1024]{2,1,0:T(8,128)(2,1)} fusion(bf16[4,512,1024]{2,1,0:T(8,128)(2,1)} %param.6, bf16[4,512]{1,0:T(4,128)(2,1)S(1)} %convert_element_type.19), kind=kLoop, calls=%fused_computation.7 | loop fusion | flops 2097152 | bytes 8392704 | tf_op jit(solution)/shard_map/mul | solution.py:104
  47.8 78.7 %all-gather.2.cloned.1.call-done = bf16[8,1024,512]{2,1,0:T(8,128)(2,1)} async-done(((bf16[1,1024,512]{2,1,0:T(8,128)(2,1)}), bf16[8,1024,512]{2,1,0:T(8,128)(2,1)}) %all-gather.2.cloned.1.call-update) | async-done | bytes 8388624 | tf_op jit(solution)/shard_map/all_gather | solution.py:115
  126.5 0.5 broadcast_in_dim.105
  127.1 1.7 copy-done
  128.7 1.9 fusion.23
  130.8 2.1 fusion.22
  133.0 1.4 copy-done.5
  134.4 0.7 fusion.20
  135.2 0.7 fusion.18
  136.0 0.7 fusion.16
  136.8 0.7 fusion.14
  137.6 0.7 fusion.12
  138.4 0.7 fusion.10
  139.1 2.4 copy.60
  141.6 8.3 %all-to-all-start = ((f32[4,32,16,512]{3,2,0,1:T(8,128)}), f32[4,32,16,512]{3,2,0,1:T(8,128)}, u32[]{:S(2)}, u32[]{:S(2)}) async-start(f32[4,32,16,512]{3,2,0,1:T(8,128)} %copy.60), calls=%async_computation | async-start | bytes 8388608 | tf_op jit(solution)/shard_map/all_to_all | solution.py:129
  149.9 2.6 copy.57
  152.4 2.3 slice_bitcast_fusion.16
  154.7 61.6 %shard_map.65 = bf16[8,1024,256]{2,1,0:T(8,128)(2,1)} custom-call(bf16[1024,256]{1,0:T(8,128)(2,1)} %get-tuple-element.13.source), custom_call_target="tpu_custom_call" | custom-call | bytes 8388608 | tf_op jit(solution)/shard_map/pallas_call | solution.py:83
  216.5 1.9 fusion.58
  218.5 0.5 copy-done.1
  219.0 1.7 fusion.43
  220.8 0.5 fusion.41
  221.8 0.4 fusion.37
  222.3 0.5 fusion.35
  223.8 3.1 copy.63
  226.9 17.0 %all-to-all-done = f32[4,32,16,512]{3,2,0,1:T(8,128)} async-done(((f32[4,32,16,512]{3,2,0,1:T(8,128)}), f32[4,32,16,512]{3,2,0,1:T(8,128)}, u32[]{:S(2)}, u32[]{:S(2)}) %all-to-all-start) | async-done | bytes 4194336 | tf_op jit(solution)/shard_map/all_to_all | solution.py:129
  243.9 6.6 %all-to-all-start.1 = ((f32[4,32,16,256]{3,0,2,1:T(4,128)}), f32[4,32,16,256]{3,0,2,1:T(4,128)S(1)}, u32[]{:S(2)}, u32[]{:S(2)}) async-start(f32[4,32,16,256]{3,0,2,1:T(4,128)} %copy.63), calls=%async_computation.1 | async-start | bytes 4194304 | tf_op jit(solution)/shard_map/all_to_all | solution.py:129
  250.5 56.4 %shard_map.64 = bf16[8,1024,256]{2,1,0:T(8,128)(2,1)} custom-call(bf16[1024,256]{1,0:T(8,128)(2,1)} %get-tuple-element.14.source), custom_call_target="tpu_custom_call" | custom-call | bytes 8388608 | tf_op jit(solution)/shard_map/pallas_call | solution.py:83
  307.1 2.0 fusion.59
  309.1 0.5 copy-done.2
  309.6 1.7 fusion.57
  311.4 0.5 fusion.55
  312.4 0.4 fusion.51
  312.9 0.5 fusion.49
  314.4 3.1 copy.66
  317.5 11.0 %all-to-all-start.2 = ((f32[4,32,16,256]{3,0,2,1:T(4,128)}), f32[4,32,16,256]{3,0,2,1:T(4,128)}, u32[]{:S(2)}, u32[]{:S(2)}) async-start(f32[4,32,16,256]{3,0,2,1:T(4,128)} %copy.66), calls=%async_computation.2 | async-start | bytes 4194304 | tf_op jit(solution)/shard_map/all_to_all | solution.py:129
  328.5 0.6 iota_reduce_fusion
  329.4 2.1 fusion.24
  331.7 6.1 %fusion.6 = f32[16,512,50]{1,2,0:T(8,128)S(1)} fusion(f32[4,32,16,512]{3,2,0,1:T(8,128)} %all-to-all-done, pred[50,4,32]{0,2,1:T(8,128)(4,1)S(1)} %and_reduce_fusion), kind=kOutput, calls=%fused_computation.9 | convolution fusion | flops 629145600 | bytes 5839104 | tf_op jit(solution)/shard_map/nsg,sgrc->rnc/dot_general | solution.py:138
  337.9 1.0 copy.87
  338.8 39.7 %all-to-all-done.2 = f32[4,32,16,256]{3,0,2,1:T(4,128)} async-done(((f32[4,32,16,256]{3,0,2,1:T(4,128)}), f32[4,32,16,256]{3,0,2,1:T(4,128)}, u32[]{:S(2)}, u32[]{:S(2)}) %all-to-all-start.2) | async-done | bytes 2097184 | tf_op jit(solution)/shard_map/all_to_all | solution.py:129
  378.5 3.7 fusion.27
  382.5 2.3 maximum_add_fusion
  (62 shorter events, 5.7 us)
Async XLA Ops:
  6.5 4.3 %copy-start.8 = (s32[8,32]{1,0:T(8,128)S(1)}, s32[8,32]{1,0:T(8,128)}, u32[]{:S(2)}) copy-start(s32[8,32]{1,0:T(8,128)} %param.10) | copy-start | bytes 3076
  6.5 4.3 %copy-start.7 = (s32[8,32]{1,0:T(8,128)S(1)}, s32[8,32]{1,0:T(8,128)}, u32[]{:S(2)}) copy-start(s32[8,32]{1,0:T(8,128)} %param.9) | copy-start | bytes 3076
  6.5 26.5 %copy-start.9 = (s32[4,32]{1,0:T(4,128)S(1)}, s32[4,32]{1,0:T(4,128)}, u32[]{:S(2)}) copy-start(s32[4,32]{1,0:T(4,128)} %param.7) | copy-start | bytes 1540
  6.5 120.0 %all-gather.2.cloned.1.call-start = ((), (), s32[]{:S(2)}) async-start(), calls=%async_computation.3 | async-start | bytes 9437184 | tf_op jit(solution)/shard_map/all_gather | solution.py:115
  126.5 2.2 copy-start
  130.7 3.7 copy-start.5
  141.6 102.4 %all-to-all-start = ((f32[4,32,16,512]{3,2,0,1:T(8,128)}), f32[4,32,16,512]{3,2,0,1:T(8,128)}, u32[]{:S(2)}, u32[]{:S(2)}) async-start(f32[4,32,16,512]{3,2,0,1:T(8,128)} %copy.60), calls=%async_computation | async-start | bytes 8388608 | tf_op jit(solution)/shard_map/all_to_all | solution.py:129
  216.3 2.7 copy-start.1
  216.3 4.5 %copy-start.4 = (bf16[8,1024,256]{2,1,0:T(8,128)(2,1)S(1)}, bf16[8,1024,256]{2,1,0:T(8,128)(2,1)}, u32[]{:S(2)}) copy-start(bf16[8,1024,256]{2,1,0:T(8,128)(2,1)} %shard_map.65) | copy-start | bytes 12582916
  243.9 73.5 %all-to-all-start.1 = ((f32[4,32,16,256]{3,0,2,1:T(4,128)}), f32[4,32,16,256]{3,0,2,1:T(4,128)S(1)}, u32[]{:S(2)}, u32[]{:S(2)}) async-start(f32[4,32,16,256]{3,0,2,1:T(4,128)} %copy.63), calls=%async_computation.1 | async-start | bytes 4194304 | tf_op jit(solution)/shard_map/all_to_all | solution.py:129
  306.9 2.7 copy-start.2
  306.9 4.5 %copy-start.3 = (bf16[8,1024,256]{2,1,0:T(8,128)(2,1)S(1)}, bf16[8,1024,256]{2,1,0:T(8,128)(2,1)}, u32[]{:S(2)}) copy-start(bf16[8,1024,256]{2,1,0:T(8,128)(2,1)} %shard_map.64) | copy-start | bytes 12582916
  317.5 61.0 %all-to-all-start.2 = ((f32[4,32,16,256]{3,0,2,1:T(4,128)}), f32[4,32,16,256]{3,0,2,1:T(4,128)}, u32[]{:S(2)}, u32[]{:S(2)}) async-start(f32[4,32,16,256]{3,0,2,1:T(4,128)} %copy.66), calls=%async_computation.2 | async-start | bytes 4194304 | tf_op jit(solution)/shard_map/all_to_all | solution.py:129
  378.5 4.0 %copy-start.6 = (f32[16,50,1024]{2,0,1:T(8,128)S(1)}, f32[16,50,1024]{2,0,1:T(8,128)}, u32[]{:S(2)}) copy-start(f32[16,50,1024]{2,0,1:T(8,128)} %param.11) | copy-start | bytes 9830404
Sparse Core Ops, SparseCore 0:
  11.0 115.4 all-gather.1

commit v12 on v11

--- a/solution.py
+++ b/solution.py
@@ -139,9 +139,10 @@
             "nsg,sgrc->rnc", onehot, arrived, precision=lax.Precision.HIGHEST, preferred_element_type=jnp.float32
         )
 
-    early = exchange(contract(gather_blk(chunked[CHUNKS // 2])))
+    early_portion, ready = lax.optimization_barrier((gather_blk(chunked[CHUNKS // 2]), offloaded))
+    early = exchange(contract(early_portion))
     late_sums = contract(gather_blk(chunked[CHUNKS - 1]))
-    offloaded_arrived = exchange(contract(offloaded))
+    offloaded_arrived = exchange(contract(ready))
     late_sums, offloaded_arrived = lax.optimization_barrier((late_sums, offloaded_arrived))
     pieces = [accumulate(offloaded_arrived), accumulate(early), accumulate(exchange(late_sums))]
     summed = jnp.concatenate(pieces, axis=2)

time: 393 us -> 395 us (level)
  Pallas kernels: 118 us -> 131 us
  waiting for transfers between devices: 135 us -> 125 us
    all_gather x1, waiting for transfers between devices: 78.7 us -> 1.5 us  [shards(): offloaded = lax.all_gather(halves[0:1], 'blk', axis=0, tiled=True)]
    all_to_all x3, waiting for transfers between devices: 56.7 us -> 123 us  [exchange(): lax.all_to_all(running.reshape(SLOTS, grp_count, owner_rows, width), 'grp...]
    pallas_call x2, Pallas kernels: 118 us -> 131 us  [gather_blk(): pl.pallas_call(functools.partial(gather_kernel, count), out_shape=jax.Sha...]
  transfers between devices with their start and end apart: 4 -> 4, of which waited for: 3 -> 3; matrix products, arithmetic and copies ran while one was open for 11% -> 11% of each run, Pallas kernels for 30% -> 33%
where the time goes in v12:
time: 395 us; the launch traced here: 394 us
  Pallas kernels  131 us (33%)
  waiting for transfers between devices  125 us (32%)
  between operations  43.9 us (11%)
  matrix products  33 us (8%)
  local copies, waits for them, and re-layouts  27 us (7%)
  starting transfers between devices  26.3 us (7%)
  other arithmetic  8.62 us (2%)
    pallas_call x2, Pallas kernels, gather_blk(): pl.pallas_call(functools.partial(gather_kernel, count), out_shape=jax.Sha...  131 us
    all_to_all x3, waiting for transfers between devices, exchange(): lax.all_to_all(running.reshape(SLOTS, grp_count, owner_rows, width), 'grp...  123 us
    all_to_all x3, starting transfers between devices, exchange(): lax.all_to_all(running.reshape(SLOTS, grp_count, owner_rows, width), 'grp...  26.3 us
    dot_general x24, matrix products, contract(): jnp.dot(rows_in, portion[offset], preferred_element_type=jnp.float32)  21.1 us
    dot_general x3, matrix products, accumulate(): jnp.einsum('nsg,sgrc->rnc', onehot, arrived, precision=lax.Precision.HIGH...  11.9 us
    reshape x3, local copies, waits for them, and re-layouts, exchange(): running.reshape(SLOTS, grp_count, owner_rows, width)  8.71 us
  transfers between devices with their start and end apart: 4, of which 3 were waited for; matrix products, arithmetic and copies ran while one was open for 11% of the time, Pallas kernels for 33%

profile of v12, /device:TPU:1, one launch (start us, length us, event | category | flops | bytes accessed | tf_op | source)
XLA Modules:
  0.0 394.0 jit_solution(15807828662806168537)
XLA Ops:
  6.5 2.9 copy.56
  9.5 1.3 copy.59
  11.1 0.7 iota_reduce_fusion.1
  12.0 0.7 fusion.187
  14.0 0.6 fusion.186
  33.5 2.6 copy.57
  36.0 2.3 slice_bitcast_fusion
  38.3 73.8 %shard_map.65 = bf16[8,1024,256]{2,1,0:T(8,128)(2,1)} custom-call(bf16[1024,256]{1,0:T(8,128)(2,1)} %get-tuple-element.17.source), custom_call_target="tpu_custom_call" | custom-call | bytes 8388608 | tf_op jit(solution)/shard_map/pallas_call | solution.py:83
  122.1 4.5 %broadcast_multiply_fusion = bf16[4,512,1024]{2,1,0:T(8,128)(2,1)} fusion(bf16[4,512,1024]{2,1,0:T(8,128)(2,1)} %param.6, bf16[4,512]{1,0:T(4,128)(2,1)S(1)} %convert_element_type.19), kind=kLoop, calls=%fused_computation.7 | loop fusion | flops 2097152 | bytes 8392704 | tf_op jit(solution)/shard_map/mul | solution.py:104
  126.6 1.5 all-gather.2.cloned.1.call-done
  128.1 0.5 broadcast_in_dim.105
  128.6 1.7 copy-done
  130.2 1.9 fusion.23
  132.3 2.1 fusion.22
  134.5 1.4 copy-done.5
  135.9 0.7 fusion.20
  136.7 0.7 fusion.18
  137.5 0.7 fusion.16
  138.3 0.7 fusion.14
  139.1 0.7 fusion.12
  139.9 0.7 fusion.10
  140.6 2.4 copy.60
  143.1 8.8 %all-to-all-start = ((f32[4,32,16,512]{3,2,0,1:T(8,128)}), f32[4,32,16,512]{3,2,0,1:T(8,128)}, u32[]{:S(2)}, u32[]{:S(2)}) async-start(f32[4,32,16,512]{3,2,0,1:T(8,128)} %copy.60), calls=%async_computation | async-start | bytes 8388608 | tf_op jit(solution)/shard_map/all_to_all | solution.py:129
  152.1 1.9 fusion.58
  154.1 0.5 copy-done.1
  154.5 1.7 fusion.43
  156.3 0.5 fusion.41
  157.9 0.5 fusion.35
  159.3 3.2 copy.63
  162.5 83.4 %all-to-all-done = f32[4,32,16,512]{3,2,0,1:T(8,128)} async-done(((f32[4,32,16,512]{3,2,0,1:T(8,128)}), f32[4,32,16,512]{3,2,0,1:T(8,128)}, u32[]{:S(2)}, u32[]{:S(2)}) %all-to-all-start) | async-done | bytes 4194336 | tf_op jit(solution)/shard_map/all_to_all | solution.py:129
  245.9 6.6 %all-to-all-start.1 = ((f32[4,32,16,256]{3,0,2,1:T(4,128)}), f32[4,32,16,256]{3,0,2,1:T(4,128)S(1)}, u32[]{:S(2)}, u32[]{:S(2)}) async-start(f32[4,32,16,256]{3,0,2,1:T(4,128)} %copy.63), calls=%async_computation.1 | async-start | bytes 4194304 | tf_op jit(solution)/shard_map/all_to_all | solution.py:129
  252.5 56.8 %shard_map.64 = bf16[8,1024,256]{2,1,0:T(8,128)(2,1)} custom-call(bf16[1024,256]{1,0:T(8,128)(2,1)} %get-tuple-element.18.source), custom_call_target="tpu_custom_call" | custom-call | bytes 8388608 | tf_op jit(solution)/shard_map/pallas_call | solution.py:83
  309.5 1.9 fusion.59
  311.5 0.5 copy-done.2
  312.0 1.7 fusion.57
  313.8 0.5 fusion.55
  314.8 0.4 fusion.51
  315.3 0.5 fusion.49
  316.3 0.4 fusion.45
  316.8 3.1 copy.66
  319.9 10.9 %all-to-all-start.2 = ((f32[4,32,16,256]{3,0,2,1:T(4,128)}), f32[4,32,16,256]{3,0,2,1:T(4,128)}, u32[]{:S(2)}, u32[]{:S(2)}) async-start(f32[4,32,16,256]{3,0,2,1:T(4,128)} %copy.66), calls=%async_computation.2 | async-start | bytes 4194304 | tf_op jit(solution)/shard_map/all_to_all | solution.py:129
  330.8 0.6 iota_reduce_fusion
  331.7 2.1 fusion.24
  334.0 6.1 %fusion.6 = f32[16,512,50]{1,2,0:T(8,128)S(1)} fusion(f32[4,32,16,512]{3,2,0,1:T(8,128)} %all-to-all-done, pred[50,4,32]{0,2,1:T(8,128)(4,1)S(1)} %and_reduce_fusion), kind=kOutput, calls=%fused_computation.9 | convolution fusion | flops 629145600 | bytes 5839104 | tf_op jit(solution)/shard_map/nsg,sgrc->rnc/dot_general | solution.py:138
  340.1 1.0 copy.87
  341.1 39.7 %all-to-all-done.2 = f32[4,32,16,256]{3,0,2,1:T(4,128)} async-done(((f32[4,32,16,256]{3,0,2,1:T(4,128)}), f32[4,32,16,256]{3,0,2,1:T(4,128)}, u32[]{:S(2)}, u32[]{:S(2)}) %all-to-all-start.2) | async-done | bytes 2097184 | tf_op jit(solution)/shard_map/all_to_all | solution.py:129
  380.8 3.7 fusion.27
  384.8 2.3 maximum_add_fusion
  (62 shorter events, 5.7 us)
Async XLA Ops:
  6.5 4.4 %copy-start.8 = (s32[8,32]{1,0:T(8,128)S(1)}, s32[8,32]{1,0:T(8,128)}, u32[]{:S(2)}) copy-start(s32[8,32]{1,0:T(8,128)} %param.10) | copy-start | bytes 3076
  6.5 4.4 %copy-start.7 = (s32[8,32]{1,0:T(8,128)S(1)}, s32[8,32]{1,0:T(8,128)}, u32[]{:S(2)}) copy-start(s32[8,32]{1,0:T(8,128)} %param.9) | copy-start | bytes 3076
  6.5 26.7 %copy-start.9 = (s32[4,32]{1,0:T(4,128)S(1)}, s32[4,32]{1,0:T(4,128)}, u32[]{:S(2)}) copy-start(s32[4,32]{1,0:T(4,128)} %param.7) | copy-start | bytes 1540
  6.5 121.5 %all-gather.2.cloned.1.call-start = ((), (), s32[]{:S(2)}) async-start(), calls=%async_computation.3 | async-start | bytes 9437184 | tf_op jit(solution)/shard_map/all_gather | solution.py:115
  128.0 2.2 copy-start
  132.2 3.7 copy-start.5
  143.1 102.9 %all-to-all-start = ((f32[4,32,16,512]{3,2,0,1:T(8,128)}), f32[4,32,16,512]{3,2,0,1:T(8,128)}, u32[]{:S(2)}, u32[]{:S(2)}) async-start(f32[4,32,16,512]{3,2,0,1:T(8,128)} %copy.60), calls=%async_computation | async-start | bytes 8388608 | tf_op jit(solution)/shard_map/all_to_all | solution.py:129
  151.9 2.7 copy-start.1
  151.9 4.5 %copy-start.3 = (bf16[8,1024,256]{2,1,0:T(8,128)(2,1)S(1)}, bf16[8,1024,256]{2,1,0:T(8,128)(2,1)}, u32[]{:S(2)}) copy-start(bf16[8,1024,256]{2,1,0:T(8,128)(2,1)} %shard_map.65) | copy-start | bytes 12582916
  245.9 74.0 %all-to-all-start.1 = ((f32[4,32,16,256]{3,0,2,1:T(4,128)}), f32[4,32,16,256]{3,0,2,1:T(4,128)S(1)}, u32[]{:S(2)}, u32[]{:S(2)}) async-start(f32[4,32,16,256]{3,0,2,1:T(4,128)} %copy.63), calls=%async_computation.1 | async-start | bytes 4194304 | tf_op jit(solution)/shard_map/all_to_all | solution.py:129
  309.3 2.7 copy-start.2
  309.3 4.5 %copy-start.4 = (bf16[8,1024,256]{2,1,0:T(8,128)(2,1)S(1)}, bf16[8,1024,256]{2,1,0:T(8,128)(2,1)}, u32[]{:S(2)}) copy-start(bf16[8,1024,256]{2,1,0:T(8,128)(2,1)} %shard_map.64) | copy-start | bytes 12582916
  319.9 60.9 %all-to-all-start.2 = ((f32[4,32,16,256]{3,0,2,1:T(4,128)}), f32[4,32,16,256]{3,0,2,1:T(4,128)}, u32[]{:S(2)}, u32[]{:S(2)}) async-start(f32[4,32,16,256]{3,0,2,1:T(4,128)} %copy.66), calls=%async_computation.2 | async-start | bytes 4194304 | tf_op jit(solution)/shard_map/all_to_all | solution.py:129
  380.8 4.0 %copy-start.6 = (f32[16,50,1024]{2,0,1:T(8,128)S(1)}, f32[16,50,1024]{2,0,1:T(8,128)}, u32[]{:S(2)}) copy-start(f32[16,50,1024]{2,0,1:T(8,128)} %param.11) | copy-start | bytes 9830404
Sparse Core Ops, SparseCore 0:
  11.0 116.9 all-gather.1

commit v13 on v12

--- a/solution.py
+++ b/solution.py
@@ -140,10 +140,11 @@
         )
 
     early_portion, ready = lax.optimization_barrier((gather_blk(chunked[CHUNKS // 2]), offloaded))
-    early = exchange(contract(early_portion))
+    early_sums = contract(early_portion)
+    offloaded_arrived = exchange(contract(ready))
+    early_sums, offloaded_arrived = lax.optimization_barrier((early_sums, offloaded_arrived))
+    early = exchange(early_sums)
     late_sums = contract(gather_blk(chunked[CHUNKS - 1]))
-    offloaded_arrived = exchange(contract(ready))
-    late_sums, offloaded_arrived = lax.optimization_barrier((late_sums, offloaded_arrived))
     pieces = [accumulate(offloaded_arrived), accumulate(early), accumulate(exchange(late_sums))]
     summed = jnp.concatenate(pieces, axis=2)
     return residual_in + summed

time: 395 us -> 374 us (0.947)
  waiting for transfers between devices: 125 us -> 104 us
  starting transfers between devices: 26.3 us -> 21.7 us
    all_to_all x3, waiting for transfers between devices: 123 us -> 102 us  [exchange(): lax.all_to_all(running.reshape(SLOTS, grp_count, owner_rows, width), 'grp...]
    all_to_all x3, starting transfers between devices: 26.3 us -> 21.7 us  [exchange(): lax.all_to_all(running.reshape(SLOTS, grp_count, owner_rows, width), 'grp...]
  transfers between devices with their start and end apart: 4 -> 4, of which waited for: 3 -> 4; matrix products, arithmetic and copies ran while one was open for 11% -> 11% of each run, Pallas kernels for 33% -> 36%
where the time goes in v13:
time: 374 us; the launch traced here: 372 us
  Pallas kernels  134 us (36%)
  waiting for transfers between devices  104 us (28%)
  between operations  44 us (12%)
  matrix products  33 us (9%)
  local copies, waits for them, and re-layouts  27 us (7%)
  starting transfers between devices  21.7 us (6%)
  other arithmetic  8.66 us (2%)
    pallas_call x2, Pallas kernels, gather_blk(): pl.pallas_call(functools.partial(gather_kernel, count), out_shape=jax.Sha...  134 us
    all_to_all x3, waiting for transfers between devices, exchange(): lax.all_to_all(running.reshape(SLOTS, grp_count, owner_rows, width), 'grp...  102 us
    all_to_all x3, starting transfers between devices, exchange(): lax.all_to_all(running.reshape(SLOTS, grp_count, owner_rows, width), 'grp...  21.7 us
    dot_general x24, matrix products, contract(): jnp.dot(rows_in, portion[offset], preferred_element_type=jnp.float32)  21.1 us
    dot_general x3, matrix products, accumulate(): jnp.einsum('nsg,sgrc->rnc', onehot, arrived, precision=lax.Precision.HIGH...  11.9 us
    reshape x3, local copies, waits for them, and re-layouts, exchange(): running.reshape(SLOTS, grp_count, owner_rows, width)  8.66 us
  transfers between devices with their start and end apart: 4, of which 4 were waited for; matrix products, arithmetic and copies ran while one was open for 11% of the time, Pallas kernels for 36%

profile of v13, /device:TPU:1, one launch (start us, length us, event | category | flops | bytes accessed | tf_op | source)
XLA Modules:
  0.0 372.1 jit_solution(3693799145865104591)
XLA Ops:
  6.5 2.9 copy.56
  9.5 1.3 copy.59
  11.1 0.6 fusion.186
  21.7 0.7 iota_reduce_fusion.1
  22.6 0.7 fusion.187
  33.6 2.6 copy.57
  36.1 2.3 slice_bitcast_fusion.1
  38.4 73.8 %shard_map.64 = bf16[8,1024,256]{2,1,0:T(8,128)(2,1)} custom-call(bf16[1024,256]{1,0:T(8,128)(2,1)} %get-tuple-element.17.source), custom_call_target="tpu_custom_call" | custom-call | bytes 8388608 | tf_op jit(solution)/shard_map/pallas_call | solution.py:83
  122.2 4.5 %broadcast_multiply_fusion = bf16[4,512,1024]{2,1,0:T(8,128)(2,1)} fusion(bf16[4,512,1024]{2,1,0:T(8,128)(2,1)} %param.6, bf16[4,512]{1,0:T(4,128)(2,1)S(1)} %convert_element_type.19), kind=kLoop, calls=%fused_computation.7 | loop fusion | flops 2097152 | bytes 8392704 | tf_op jit(solution)/shard_map/mul | solution.py:104
  126.7 1.5 all-gather.2.cloned.1.call-done
  128.1 0.5 broadcast_in_dim.105
  128.7 1.7 copy-done
  130.3 1.9 fusion.23
  132.4 2.1 fusion.22
  134.6 1.4 copy-done.5
  136.0 0.7 fusion.20
  136.8 0.7 fusion.18
  137.6 0.7 fusion.16
  138.4 0.7 fusion.14
  139.2 0.7 fusion.12
  140.0 0.7 fusion.10
  140.7 2.4 copy.60
  143.2 8.8 %all-to-all-start = ((f32[4,32,16,512]{3,2,0,1:T(8,128)}), f32[4,32,16,512]{3,2,0,1:T(8,128)}, u32[]{:S(2)}, u32[]{:S(2)}) async-start(f32[4,32,16,512]{3,2,0,1:T(8,128)} %copy.60), calls=%async_computation | async-start | bytes 8388608 | tf_op jit(solution)/shard_map/all_to_all | solution.py:129
  151.9 60.4 %shard_map.65 = bf16[8,1024,256]{2,1,0:T(8,128)(2,1)} custom-call(bf16[1024,256]{1,0:T(8,128)(2,1)} %get-tuple-element.18.source), custom_call_target="tpu_custom_call" | custom-call | bytes 8388608 | tf_op jit(solution)/shard_map/pallas_call | solution.py:83
  212.6 2.0 fusion.58
  214.6 0.5 copy-done.1
  215.0 1.7 fusion.43
  217.4 0.5 fusion.39
  217.9 0.5 fusion.37
  219.4 0.5 fusion.31
  219.9 3.1 copy.66
  223.0 23.1 %all-to-all-done = f32[4,32,16,512]{3,2,0,1:T(8,128)} async-done(((f32[4,32,16,512]{3,2,0,1:T(8,128)}), f32[4,32,16,512]{3,2,0,1:T(8,128)}, u32[]{:S(2)}, u32[]{:S(2)}) %all-to-all-start) | async-done | bytes 4194336 | tf_op jit(solution)/shard_map/all_to_all | solution.py:129
  246.0 6.6 %all-to-all-start.2 = ((f32[4,32,16,256]{3,0,2,1:T(4,128)}), f32[4,32,16,256]{3,0,2,1:T(4,128)S(1)}, u32[]{:S(2)}, u32[]{:S(2)}) async-start(f32[4,32,16,256]{3,0,2,1:T(4,128)} %copy.66), calls=%async_computation.2 | async-start | bytes 4194304 | tf_op jit(solution)/shard_map/all_to_all | solution.py:129
  252.8 2.0 fusion.59
  254.8 0.5 copy-done.2
  255.3 1.7 fusion.57
  258.1 0.5 fusion.51
  259.6 0.5 fusion.45
  260.1 3.1 copy.63
  263.2 39.5 %all-to-all-done.2 = f32[4,32,16,256]{3,0,2,1:T(4,128)S(1)} async-done(((f32[4,32,16,256]{3,0,2,1:T(4,128)}), f32[4,32,16,256]{3,0,2,1:T(4,128)S(1)}, u32[]{:S(2)}, u32[]{:S(2)}) %all-to-all-start.2) | async-done | bytes 2097184 | tf_op jit(solution)/shard_map/all_to_all | solution.py:129
  302.7 6.3 %all-to-all-start.1 = ((f32[4,32,16,256]{3,0,2,1:T(4,128)}), f32[4,32,16,256]{3,0,2,1:T(4,128)}, u32[]{:S(2)}, u32[]{:S(2)}) async-start(f32[4,32,16,256]{3,0,2,1:T(4,128)} %copy.63), calls=%async_computation.1 | async-start | bytes 4194304 | tf_op jit(solution)/shard_map/all_to_all | solution.py:129
  309.0 0.6 iota_reduce_fusion
  310.0 2.1 fusion.27
  312.4 6.1 %fusion.6 = f32[16,512,50]{1,2,0:T(8,128)S(1)} fusion(f32[4,32,16,512]{3,2,0,1:T(8,128)} %all-to-all-done, pred[50,4,32]{0,2,1:T(8,128)(4,1)S(1)} %and_reduce_fusion), kind=kOutput, calls=%fused_computation.9 | convolution fusion | flops 629145600 | bytes 5839104 | tf_op jit(solution)/shard_map/nsg,sgrc->rnc/dot_general | solution.py:138
  318.5 1.0 copy.87
  319.4 39.5 %all-to-all-done.1 = f32[4,32,16,256]{3,0,2,1:T(4,128)} async-done(((f32[4,32,16,256]{3,0,2,1:T(4,128)}), f32[4,32,16,256]{3,0,2,1:T(4,128)}, u32[]{:S(2)}, u32[]{:S(2)}) %all-to-all-start.1) | async-done | bytes 2097184 | tf_op jit(solution)/shard_map/all_to_all | solution.py:129
  359.0 3.7 fusion.24
  362.9 2.3 maximum_add_fusion
  (62 shorter events, 6.2 us)
Async XLA Ops:
  6.5 4.4 %copy-start.7 = (s32[8,32]{1,0:T(8,128)S(1)}, s32[8,32]{1,0:T(8,128)}, u32[]{:S(2)}) copy-start(s32[8,32]{1,0:T(8,128)} %param.9) | copy-start | bytes 3076
  6.5 4.4 %copy-start.8 = (s32[8,32]{1,0:T(8,128)S(1)}, s32[8,32]{1,0:T(8,128)}, u32[]{:S(2)}) copy-start(s32[8,32]{1,0:T(8,128)} %param.10) | copy-start | bytes 3076
  6.5 26.8 %copy-start.9 = (s32[4,32]{1,0:T(4,128)S(1)}, s32[4,32]{1,0:T(4,128)}, u32[]{:S(2)}) copy-start(s32[4,32]{1,0:T(4,128)} %param.7) | copy-start | bytes 1540
  6.5 121.6 %all-gather.2.cloned.1.call-start = ((), (), s32[]{:S(2)}) async-start(), calls=%async_computation.3 | async-start | bytes 9437184 | tf_op jit(solution)/shard_map/all_gather | solution.py:115
  128.1 2.2 copy-start
  132.3 3.7 copy-start.5
  143.2 102.9 %all-to-all-start = ((f32[4,32,16,512]{3,2,0,1:T(8,128)}), f32[4,32,16,512]{3,2,0,1:T(8,128)}, u32[]{:S(2)}, u32[]{:S(2)}) async-start(f32[4,32,16,512]{3,2,0,1:T(8,128)} %copy.60), calls=%async_computation | async-start | bytes 8388608 | tf_op jit(solution)/shard_map/all_to_all | solution.py:129
  212.4 2.7 copy-start.1
  212.4 4.5 %copy-start.4 = (bf16[8,1024,256]{2,1,0:T(8,128)(2,1)S(1)}, bf16[8,1024,256]{2,1,0:T(8,128)(2,1)}, u32[]{:S(2)}) copy-start(bf16[8,1024,256]{2,1,0:T(8,128)(2,1)} %shard_map.65) | copy-start | bytes 12582916
  246.0 56.7 %all-to-all-start.2 = ((f32[4,32,16,256]{3,0,2,1:T(4,128)}), f32[4,32,16,256]{3,0,2,1:T(4,128)S(1)}, u32[]{:S(2)}, u32[]{:S(2)}) async-start(f32[4,32,16,256]{3,0,2,1:T(4,128)} %copy.66), calls=%async_computation.2 | async-start | bytes 4194304 | tf_op jit(solution)/shard_map/all_to_all | solution.py:129
  252.6 2.7 copy-start.2
  252.6 4.5 %copy-start.3 = (bf16[8,1024,256]{2,1,0:T(8,128)(2,1)S(1)}, bf16[8,1024,256]{2,1,0:T(8,128)(2,1)}, u32[]{:S(2)}) copy-start(bf16[8,1024,256]{2,1,0:T(8,128)(2,1)} %shard_map.64) | copy-start | bytes 12582916
  302.7 56.3 %all-to-all-start.1 = ((f32[4,32,16,256]{3,0,2,1:T(4,128)}), f32[4,32,16,256]{3,0,2,1:T(4,128)}, u32[]{:S(2)}, u32[]{:S(2)}) async-start(f32[4,32,16,256]{3,0,2,1:T(4,128)} %copy.63), calls=%async_computation.1 | async-start | bytes 4194304 | tf_op jit(solution)/shard_map/all_to_all | solution.py:129
  359.0 4.0 %copy-start.6 = (f32[16,50,1024]{2,0,1:T(8,128)S(1)}, f32[16,50,1024]{2,0,1:T(8,128)}, u32[]{:S(2)}) copy-start(f32[16,50,1024]{2,0,1:T(8,128)} %param.11) | copy-start | bytes 9830404
Sparse Core Ops, SparseCore 0:
  11.0 117.0 all-gather.1

commit v14 on v13

--- a/solution.py
+++ b/solution.py
@@ -143,9 +143,8 @@
     early_sums = contract(early_portion)
     offloaded_arrived = exchange(contract(ready))
     early_sums, offloaded_arrived = lax.optimization_barrier((early_sums, offloaded_arrived))
-    early = exchange(early_sums)
     late_sums = contract(gather_blk(chunked[CHUNKS - 1]))
-    pieces = [accumulate(offloaded_arrived), accumulate(early), accumulate(exchange(late_sums))]
+    pieces = [accumulate(offloaded_arrived), accumulate(exchange(jnp.concatenate([early_sums, late_sums], axis=2)))]
     summed = jnp.concatenate(pieces, axis=2)
     return residual_in + summed
 

time: 374 us -> 389 us (1.040)
  waiting for transfers between devices: 104 us -> 87.5 us
  local copies, waits for them, and re-layouts: 27 us -> 43.2 us
  matrix products: 33 us -> 43.2 us
    all_to_all x3 -> x2, waiting for transfers between devices: 102 us -> 86 us  [exchange(): lax.all_to_all(running.reshape(SLOTS, grp_count, owner_rows, width), 'grp...]
    dot_general x24, matrix products: 21.1 us -> 30.5 us  [contract(): jnp.dot(rows_in, portion[offset], preferred_element_type=jnp.float32)]
    dynamic_slice x21 -> x28, local copies, waits for them, and re-layouts: 1.15 us -> 9.74 us  [contract(): earlier = lax.dynamic_index_in_dim(running, slot, 0, keepdims=False)]
    dynamic_update_slice x0 -> x7, local copies, waits for them, and re-layouts: none -> 5.83 us  [contract(): lax.dynamic_update_index_in_dim(running, earlier + product, slot, 0)]
    all_to_all x3 -> x2, starting transfers between devices: 21.7 us -> 23.5 us  [exchange(): lax.all_to_all(running.reshape(SLOTS, grp_count, owner_rows, width), 'grp...]
    dot_general x3 -> x2, matrix products: 11.9 us -> 12.7 us  [accumulate(): jnp.einsum('nsg,sgrc->rnc', onehot, arrived, precision=lax.Precision.HIGH...]
    reshape x3 -> x2, local copies, waits for them, and re-layouts: 8.66 us -> 8.22 us  [exchange(): running.reshape(SLOTS, grp_count, owner_rows, width)]
  transfers between devices with their start and end apart: 4 -> 3, of which waited for: 4 -> 2; matrix products, arithmetic and copies ran while one was open for 11% -> 16% of each run, Pallas kernels for 36% -> 35%
where the time goes in v14:
time: 389 us; the launch traced here: 386 us
  Pallas kernels  134 us (34%)
  waiting for transfers between devices  87.5 us (22%)
  between operations  44.1 us (11%)
  local copies, waits for them, and re-layouts  43.2 us (11%)
  matrix products  43.2 us (11%)
  starting transfers between devices  23.5 us (6%)
  other arithmetic  10.9 us (3%)
    pallas_call x2, Pallas kernels, gather_blk(): pl.pallas_call(functools.partial(gather_kernel, count), out_shape=jax.Sha...  134 us
    all_to_all x2, waiting for transfers between devices, exchange(): lax.all_to_all(running.reshape(SLOTS, grp_count, owner_rows, width), 'grp...  86 us
    dot_general x24, matrix products, contract(): jnp.dot(rows_in, portion[offset], preferred_element_type=jnp.float32)  30.5 us
    all_to_all x2, starting transfers between devices, exchange(): lax.all_to_all(running.reshape(SLOTS, grp_count, owner_rows, width), 'grp...  23.5 us
    dot_general x2, matrix products, accumulate(): jnp.einsum('nsg,sgrc->rnc', onehot, arrived, precision=lax.Precision.HIGH...  12.7 us
    dynamic_slice x28, local copies, waits for them, and re-layouts, contract(): earlier = lax.dynamic_index_in_dim(running, slot, 0, keepdims=False)  9.74 us
    reshape x2, local copies, waits for them, and re-layouts, exchange(): running.reshape(SLOTS, grp_count, owner_rows, width)  8.22 us
  transfers between devices with their start and end apart: 3, of which 2 were waited for; matrix products, arithmetic and copies ran while one was open for 16% of the time, Pallas kernels for 35%

profile of v14, /device:TPU:1, one launch (start us, length us, event | category | flops | bytes accessed | tf_op | source)
XLA Modules:
  0.0 386.5 jit_solution(15836420621492706014)
XLA Ops:
  6.5 2.9 copy.125
  9.5 1.3 copy.128
  33.5 2.6 copy.126
  36.1 2.3 slice_bitcast_fusion.1
  38.4 73.8 %shard_map.64 = bf16[8,1024,256]{2,1,0:T(8,128)(2,1)} custom-call(bf16[1024,256]{1,0:T(8,128)(2,1)} %get-tuple-element.17.source), custom_call_target="tpu_custom_call" | custom-call | bytes 8388608 | tf_op jit(solution)/shard_map/pallas_call | solution.py:83
  122.2 4.5 %broadcast_multiply_fusion = bf16[4,512,1024]{2,1,0:T(8,128)(2,1)} fusion(bf16[4,512,1024]{2,1,0:T(8,128)(2,1)} %param.6, bf16[4,512]{1,0:T(4,128)(2,1)S(1)} %convert_element_type.19), kind=kLoop, calls=%fused_computation.6 | loop fusion | flops 2097152 | bytes 8392704 | tf_op jit(solution)/shard_map/mul | solution.py:104
  126.7 1.5 all-gather.2.cloned.1.call-done
  128.7 1.7 copy-done
  130.3 1.9 fusion.24
  132.4 2.1 fusion.23
  134.5 1.4 copy-done.3
  140.7 2.4 copy.129
  143.1 8.8 %all-to-all-start = ((f32[4,32,16,512]{3,2,0,1:T(8,128)}), f32[4,32,16,512]{3,2,0,1:T(8,128)}, u32[]{:S(2)}, u32[]{:S(2)}) async-start(f32[4,32,16,512]{3,2,0,1:T(8,128)} %copy.129), calls=%async_computation | async-start | bytes 8388608 | tf_op jit(solution)/shard_map/all_to_all | solution.py:129
  151.9 60.4 %shard_map.65 = bf16[8,1024,256]{2,1,0:T(8,128)(2,1)} custom-call(bf16[1024,256]{1,0:T(8,128)(2,1)} %get-tuple-element.18.source), custom_call_target="tpu_custom_call" | custom-call | bytes 8388608 | tf_op jit(solution)/shard_map/pallas_call | solution.py:83
  212.4 1.5 broadcast.27.clone
  213.9 2.6 fusion.46
  216.5 1.1 constant_dynamic-slice_fusion.6
  217.8 1.8 fusion.31
  219.8 0.8 constant_dynamic-update-slice_fusion.6
  220.6 1.1 constant_dynamic-slice_fusion.5
  221.9 1.8 fusion.30
  224.0 0.8 constant_dynamic-update-slice_fusion.5
  224.8 1.1 constant_dynamic-slice_fusion.4
  226.1 1.8 fusion.29
  228.2 0.8 constant_dynamic-update-slice_fusion.4
  229.0 1.1 constant_dynamic-slice_fusion.3
  230.3 1.8 fusion.28
  232.3 0.8 constant_dynamic-update-slice_fusion.3
  233.2 1.1 constant_dynamic-slice_fusion.2
  234.5 1.8 fusion.27
  236.5 0.8 constant_dynamic-update-slice_fusion.2
  237.4 1.1 constant_dynamic-slice_fusion.1
  238.6 1.8 fusion.26
  240.7 0.8 constant_dynamic-update-slice_fusion.1
  241.5 1.1 constant_dynamic-slice_fusion
  242.8 1.8 fusion.25
  244.9 0.8 constant_dynamic-update-slice_fusion
  245.9 2.5 fusion.47
  248.4 1.5 fusion.45
  252.9 2.1 pad_maximum_fusion
  255.1 5.8 %copy.147 = f32[4,32,16,512]{3,0,2,1:T(4,128)} copy(f32[4,32,16,512]{3,2,1,0:T(8,128)S(1)} %bitcast.298) | data formatting | bytes 8388608 | tf_op jit(solution)/shard_map/reshape | solution.py:130
  260.9 14.7 %all-to-all-start.1 = ((f32[4,32,16,512]{3,0,2,1:T(4,128)}), f32[4,32,16,512]{3,0,2,1:T(4,128)}, u32[]{:S(2)}, u32[]{:S(2)}) async-start(f32[4,32,16,512]{3,0,2,1:T(4,128)} %copy.147), calls=%async_computation.1 | async-start | bytes 8388608 | tf_op jit(solution)/shard_map/all_to_all | solution.py:129
  276.5 6.1 %fusion.4 = f32[16,512,50]{1,2,0:T(8,128)S(1)} fusion(f32[4,32,16,512]{3,2,0,1:T(8,128)} %all-to-all-done, pred[50,4,32]{0,2,1:T(8,128)(4,1)S(1)} %and_reduce_fusion), kind=kOutput, calls=%fused_computation.9 | convolution fusion | flops 629145600 | bytes 5839104 | tf_op jit(solution)/shard_map/nsg,sgrc->rnc/dot_general | solution.py:138
  282.7 1.0 copy.163
  283.6 86.0 %all-to-all-done.1 = f32[4,32,16,512]{3,0,2,1:T(4,128)} async-done(((f32[4,32,16,512]{3,0,2,1:T(4,128)}), f32[4,32,16,512]{3,0,2,1:T(4,128)}, u32[]{:S(2)}, u32[]{:S(2)}) %all-to-all-start.1) | async-done | bytes 4194336 | tf_op jit(solution)/shard_map/all_to_all | solution.py:129
  369.6 6.6 %fusion.7 = f32[16,512,50]{1,2,0:T(8,128)S(1)} fusion(f32[4,32,16,512]{3,0,2,1:T(4,128)} %all-to-all-done.1, pred[50,4,32]{0,2,1:T(8,128)(4,1)S(1)} %and_reduce_fusion), kind=kOutput, calls=%fused_computation.10 | convolution fusion | flops 629145600 | bytes 5839104 | tf_op jit(solution)/shard_map/nsg,sgrc->rnc/dot_general | solution.py:138
  376.3 1.0 copy.162
  377.2 2.4 maximum_add_fusion
  (75 shorter events, 14.9 us)
Async XLA Ops:
  6.5 4.4 %copy-start.6 = (s32[8,32]{1,0:T(8,128)S(1)}, s32[8,32]{1,0:T(8,128)}, u32[]{:S(2)}) copy-start(s32[8,32]{1,0:T(8,128)} %param.10) | copy-start | bytes 3076
  6.5 4.4 %copy-start.5 = (s32[8,32]{1,0:T(8,128)S(1)}, s32[8,32]{1,0:T(8,128)}, u32[]{:S(2)}) copy-start(s32[8,32]{1,0:T(8,128)} %param.9) | copy-start | bytes 3076
  6.5 26.8 %copy-start.7 = (s32[4,32]{1,0:T(4,128)S(1)}, s32[4,32]{1,0:T(4,128)}, u32[]{:S(2)}) copy-start(s32[4,32]{1,0:T(4,128)} %param.7) | copy-start | bytes 1540
  6.5 121.6 %all-gather.2.cloned.1.call-start = ((), (), s32[]{:S(2)}) async-start(), calls=%async_computation.2 | async-start | bytes 9437184 | tf_op jit(solution)/shard_map/all_gather | solution.py:115
  128.1 2.2 copy-start
  132.3 3.7 copy-start.3
  143.1 109.8 %all-to-all-start = ((f32[4,32,16,512]{3,2,0,1:T(8,128)}), f32[4,32,16,512]{3,2,0,1:T(8,128)}, u32[]{:S(2)}, u32[]{:S(2)}) async-start(f32[4,32,16,512]{3,2,0,1:T(8,128)} %copy.129), calls=%async_computation | async-start | bytes 8388608 | tf_op jit(solution)/shard_map/all_to_all | solution.py:129
  244.9 3.5 copy-start.1
  245.7 4.2 %copy-start.2 = (bf16[8,1024,256]{2,1,0:T(8,128)(2,1)S(1)}, bf16[8,1024,256]{2,1,0:T(8,128)(2,1)}, u32[]{:S(2)}) copy-start(bf16[8,1024,256]{2,1,0:T(8,128)(2,1)} %shard_map.64) | copy-start | bytes 12582916
  260.9 108.8 %all-to-all-start.1 = ((f32[4,32,16,512]{3,0,2,1:T(4,128)}), f32[4,32,16,512]{3,0,2,1:T(4,128)}, u32[]{:S(2)}, u32[]{:S(2)}) async-start(f32[4,32,16,512]{3,0,2,1:T(4,128)} %copy.147), calls=%async_computation.1 | async-start | bytes 8388608 | tf_op jit(solution)/shard_map/all_to_all | solution.py:129
  369.6 7.6 %copy-start.4 = (f32[16,50,1024]{2,0,1:T(8,128)S(1)}, f32[16,50,1024]{2,0,1:T(8,128)}, u32[]{:S(2)}) copy-start(f32[16,50,1024]{2,0,1:T(8,128)} %param.11) | copy-start | bytes 9830404
Sparse Core Ops, SparseCore 0:
  11.0 117.0 all-gather.1
